TPU v7x, 256 devices: a whole 4x4x8 slice. The times are simulated.
256 devices in a mesh: pb: 32 (over x, y, z_lo), row: 8 (over z_hi, core).
Axes of the slice: x: 4, y: 4, z: 8 (z_hi: 4, z_lo: 2; z = z_hi * 2 + z_lo), core: 2. Of those that a mesh axis runs over, the one named last changes fastest.
Arguments:
- query_desc: bfloat16 [16384, 512], P(('pb', 'row')), may hold values from -6 to 6
- ref_desc: bfloat16 [12288, 512], P(('row', 'pb')), may hold values from -6 to 6
- taps: float32 [2, 8], replicated, may hold values from -1.3 to 1.3
Outputs:
- aligned: float32 [16384, 12288], P('pb', 'row')
All inputs are finite; a program needn't handle non-finite values.
Results may differ from a plain program's by a relative error of at most 0.0003.
Values may be sent and summed in bfloat16 or wider, within the bound.
No kernel may reach another device: no remote copies, remote signals or barrier semaphores. Data moves between devices by JAX's collectives and lax.ppermute only.
A program may use at most 64 MiB of HBM per device.

v0:
```python
import jax
import jax.numpy as jnp
import numpy as np
from jax import lax
from jax.experimental import pallas as pl
from jax.experimental.pallas import tpu as pltpu
from jax.sharding import Mesh, PartitionSpec as P

D = 32
K = 8
DESC = 512
NB = 30
PB = ("x", "y", "zl")
ROW = ("zh", "c")
SIZES = (4, 4, 2, 4, 2)


def arrange(slot_a, slot_b, slot_c, slot_d, place_ref, refs, send_left, send_right):
    core, second = place_ref[1], place_ref[2]
    inner = jnp.where(core == 0, 384, 96)
    outer = jnp.where(core == 0, 96, 384)
    for s, ref in enumerate((slot_a, slot_b, slot_c, slot_d)):
        at = lax.rem(second - s + 4, 4) * outer
        for i in range(4):
            refs[pl.ds(pl.multiple_of(at + i * inner, 96), 96), :] = ref[i * 96:i * 96 + 96, :]
    send_left[...] = refs[1280:1536, :]
    send_right[...] = refs[0:192, :]


def score_tiles(qs, base, rhs, first, count):
    scale = DESC ** -0.5
    for c in range(4):
        us = range(c, NB, 4)
        lhs = jnp.concatenate([qs[u * D:(u + 1) * D, :] for u in us], axis=0)
        s = lax.dot_general(lhs, rhs(c), (((1,), (1,)), ((), ())), preferred_element_type=jnp.float32)
        s = jnp.tanh(s * scale)
        for h in range(count):
            for n, u in enumerate(us):
                for v in range(4):
                    base[first + h, v, u] = s[n * D + v * 8:n * D + v * 8 + 8, h * 128:h * 128 + 128]


def make_diagonals(base, res, taps_ref, flag_ref, cmask):
    lane = lax.broadcasted_iota(jnp.int32, (8, 128), 1)

    def filters(p):
        w = [taps_ref[p, k] for k in range(K)]
        even, odd = w[0::2], w[1::2]
        return even, odd, [a + b for a, b in zip(even, odd)]


    def total(w, vals):
        p = [a * b for a, b in zip(w, vals)]
        return (p[0] + p[1]) + (p[2] + p[3])

    banks = [filters(0), filters(1)]

    def taps_of(bank, x):
        even, odd, both = bank
        memo = {}

        def once(key, fn):
            if key not in memo:
                memo[key] = fn()
            return memo[key]

        def pair(n):
            return once(("s", n), lambda: x(2 * n) + x(2 * n - 1))

        def a(n):
            return once(("a", n), lambda: total(even, [x(2 * (n + j - 2)) for j in range(4)]))

        def b(n):
            return once(("b", n), lambda: total(odd, [x(2 * (n + j - 2) - 1) for j in range(4)]))

        def y(u):
            if u % 2 == 0:
                return a(u // 2) + b(u // 2 + 1)
            n = (u + 1) // 2
            return total(both, [pair(n + j - 2) for j in range(4)]) - (a(n) + b(n))

        return y

    def chain(m, v, lo, hi, masked):
        a0 = (lo - 8) // 4
        d_view = base.at[pl.ds(m + a0 + 1, (hi + 6) // 4 - a0 + 1), v]
        m_view = cmask.at[pl.ds(m + a0 + 1, (hi + 6) // 4 - a0 + 1)] if masked else None
        o_view = res.at[pl.ds(m + lo // 4 - 1, (hi - lo) // 4 + 2), pl.ds(pl.multiple_of(v * 8, 8), 488)]
        d, f = {}, {}

        def load(u):
            if u not in d:
                d[u] = d_view[u // 4 - a0, u]
            return d[u]

        y0 = taps_of(banks[0], load)
        y1 = taps_of(banks[1], f.__getitem__)
        for u in range(lo - 4, hi + 4):
            x = jnp.tanh(y0(u))
            if masked:
                x = x * m_view[u // 4 - a0, u % 4]
            if u < 8:
                x = x * flag_ref[0]
            if u >= 24:
                x = x * flag_ref[1]
            f[u] = x
            w = u - 3
            if w >= lo:
                o = jnp.tanh(y1(w))
                c, at, r = w % 4, w // 4 - lo // 4, (w - 8) * D
                if c == 0:
                    o_view[at, r:r + 8] = o
                else:
                    o = pltpu.roll(o, 32 * c, 1)
                    pltpu.store(o_view.at[at, r:r + 8], o, mask=lane >= 32 * c)
                    pltpu.store(o_view.at[at + 1, r:r + 8], o, mask=lane < 32 * c)

    def diagonals(m0, m1, lo, hi, masked, after=None):
        def step(m, _):
            for v in range(4):
                chain(m, v, lo, hi, masked)
            if after is not None:
                after(m)
            return 0

        lax.fori_loop(m0, m1, step, 0)

    return diagonals


def middle(mine_ref, other_ref, refs_ref, taps_ref, flag_ref, place_ref, qs, base, res):
    zh, core = place_ref[0], place_ref[1]
    for s in range(4):
        for ref, c in ((mine_ref, core), (other_ref, 1 - core)):
            w = 2 * lax.rem(zh - s + 4, 4) + c
            qs[pl.ds(pl.multiple_of(256 + w * 64, 64), 64), :] = ref[s * 128:s * 128 + 64, :]
            rim = jnp.where(w >= 4, (w - 4) * 64, 768 + w * 64)
            qs[pl.ds(pl.multiple_of(rim, 64), 64), :] = ref[s * 128 + 64:s * 128 + 128, :]

    def rows(start, size):
        return lambda c: refs_ref[pl.ds(pl.multiple_of(start + c * D, D), size), :]

    def pair(i, _):
        score_tiles(qs, base, rows(i * 256, 256), 3 + 2 * i, 2)
        return 0

    lax.fori_loop(0, 5, pair, 0)
    score_tiles(qs, base, rows(1280, 128), 13, 1)
    make_diagonals(base, res, taps_ref, flag_ref, None)(2, 6, 8, 23, False)


def edges(base_in, res_in, qs, refs_ref, left_ref, right_ref, taps_ref, flag_ref,
          base, res, o_ref, lo_rows, hi_rows, cmask, sems):
    lo_rows[0:128, :] = jnp.zeros((128, DESC), lo_rows.dtype)
    lo_rows[128:384, :] = left_ref[...]
    lo_rows[384:512, :] = refs_ref[0:128, :]
    hi_rows[0:128, :] = refs_ref[1408:1536, :]
    hi_rows[128:320, :] = right_ref[...]
    hi_rows[320:512, :] = jnp.zeros((192, DESC), hi_rows.dtype)
    for rows, first in ((lo_rows, 0), (hi_rows, 14)):
        score_tiles(qs, base, lambda c: rows[c * D:c * D + 384, :], first, 3)
    j = lax.broadcasted_iota(jnp.int32, (8, 128), 1) - 128
    for t in range(17):
        for c in range(4):
            jt = j + (t * 128 + c * D)
            cmask[t, c] = jnp.where(jt < 256, flag_ref[2], jnp.where(jt >= 1792, flag_ref[3], 1.0))

    def out_copy(n):
        return pltpu.make_async_copy(
            res.at[n + 1], o_ref.at[:, pl.ds(pl.multiple_of(n * 128, 128), 128)], sems.at[n])

    def send(m):
        out_copy(m).start()

    diagonals = make_diagonals(base, res, taps_ref, flag_ref, cmask)
    diagonals(-4, -3, 20, 23, True)
    diagonals(-3, -2, 16, 23, True)
    diagonals(-2, -1, 12, 23, True)
    diagonals(-1, 0, 8, 23, True)
    diagonals(0, 2, 8, 23, True, send)
    for n in range(2, 6):
        send(n)
    diagonals(6, 9, 8, 23, True, send)
    diagonals(9, 10, 8, 19, True, send)
    diagonals(10, 11, 8, 15, True, send)
    diagonals(11, 12, 8, 11, True, send)
    for n in range(12):
        out_copy(n).wait()


VMEM = pl.BlockSpec(memory_space=pltpu.VMEM)
SMEM = pl.BlockSpec(memory_space=pltpu.SMEM)


def rows_of(n):
    return jax.ShapeDtypeStruct((n, DESC), jnp.bfloat16)


def f32(*shape):
    return jax.ShapeDtypeStruct(shape, jnp.float32)


def params(mib):
    return pltpu.CompilerParams(vmem_limit_bytes=mib << 20)


def cost(flops, size):
    return pl.CostEstimate(flops=flops, bytes_accessed=size, transcendentals=0)


BASE, RES = (17, 4, NB, 8, 128), (14, 512, 128)


def pack(a, b, c, d, stack):
    for s, ref in enumerate((a, b, c, d)):
        stack[s * 128:s * 128 + 128, :] = ref[...]


def run_pack(parts):
    return pl.pallas_call(
        pack, out_shape=rows_of(512), in_specs=[VMEM] * 4, out_specs=VMEM,
        compiler_params=params(4), cost_estimate=cost(0, 1 << 20))(*parts)


def run_arrange(slots, place):
    return pl.pallas_call(
        arrange, out_shape=[rows_of(1536), rows_of(256), rows_of(192)],
        in_specs=[VMEM] * 4 + [SMEM], out_specs=[VMEM] * 3,
        compiler_params=params(8), cost_estimate=cost(0, 3 << 20))(*slots, place)


def run_middle(mine, other, refs, taps, flags, place):
    return pl.pallas_call(
        middle, out_shape=[rows_of(1024), f32(*BASE), f32(*RES)],
        in_specs=[VMEM] * 3 + [SMEM] * 3, out_specs=[VMEM] * 3,
        compiler_params=params(20), cost_estimate=cost(1 << 32, 12 << 20))(mine, other, refs, taps, flags, place)


def run_edges(base, res, qs, refs, left, right, taps, flags):
    return pl.pallas_call(
        edges, out_shape=[f32(*BASE), f32(*RES), f32(512, 1536)],
        in_specs=[VMEM] * 6 + [SMEM] * 2, out_specs=[VMEM] * 2 + [pl.BlockSpec(memory_space=pl.ANY)],
        scratch_shapes=[pltpu.VMEM((512, DESC), jnp.bfloat16), pltpu.VMEM((512, DESC), jnp.bfloat16),
                        pltpu.VMEM((17, 4, 8, 128), jnp.float32), pltpu.SemaphoreType.DMA((12,))],
        input_output_aliases={0: 0, 1: 1},
        compiler_params=params(20), cost_estimate=cost(1 << 32, 12 << 20))(base, res, qs, refs, left, right, taps, flags)[2]


def move_rows(value, move):
    pairs = []
    for src in np.ndindex(*SIZES):
        dst = move(*src)
        if dst is not None:
            pairs.append((int(np.ravel_multi_index(src, SIZES)), int(np.ravel_multi_index(dst, SIZES))))
    return lax.ppermute(value, PB + ROW, pairs)


def rim_of_queries(x, y, zl, zh, c):
    p, w = (x * 4 + y) * 2 + zl, zh * 2 + c
    p = p + 1 if w >= 4 else p - 1
    return None if p < 0 or p > 31 else (p // 8, p // 2 % 4, p % 2, zh, c)


def along_second(d):
    def move(x, y, zl, zh, c):
        return (x, (y + d) % 4, zl, zh, c) if c == 0 else ((x + d) % 4, y, zl, zh, c)

    return move


def first_groups():
    at = lambda *i: int(np.ravel_multi_index(i, (4, 4, 2, 2)))
    rows = [[at(x, y, z, 0) for x in range(4) for z in range(2)] for y in range(4)]
    return rows + [[at(x, y, z, 1) for y in range(4) for z in range(2)] for x in range(4)]


def local(q, r, taps):
    index = {a: lax.axis_index(a) for a in PB + ROW}
    pb, row = lax.axis_index(PB), lax.axis_index(ROW)
    second = jnp.where(index["c"] == 0, index["y"], index["x"])
    flags = jnp.stack([pb != 0, pb != 31, row != 0, row != 7]).astype(jnp.float32)
    place = jnp.stack([index["zh"], index["c"], second])

    rim = move_rows(q, rim_of_queries)
    block = lax.all_to_all(jnp.broadcast_to(r[None], (8, 48, DESC)), PB + ("c",), 0, 0,
                           axis_index_groups=first_groups(), tiled=True).reshape(384, DESC)
    both = jnp.concatenate([q, rim], axis=0)
    turned = [lax.ppermute(both, "zh", [(i, (i + d) % 4) for i in range(4)]) for d in (1, 2, 3)]
    stack = run_pack([both] + turned)
    other = lax.ppermute(stack, "c", [(0, 1), (1, 0)])
    slots = [block] + [move_rows(block, along_second(d)) for d in (1, 2, 3)]
    refs, send_left, send_right = run_arrange(slots, place)
    left = lax.ppermute(send_left, ROW, [(i, i + 1) for i in range(7)])
    right = lax.ppermute(send_right, ROW, [(i + 1, i) for i in range(7)])
    qs, base, res = run_middle(stack, other, refs, taps, flags, place)
    return run_edges(base, res, qs, refs, left, right, taps, flags)


def solution(mesh):
    split = Mesh(mesh.devices.reshape(SIZES), PB + ROW)
    specs = (P(PB + ROW, None), P(ROW + PB, None), P())
    return jax.shard_map(local, mesh=split, in_specs=specs, out_specs=P(PB, ROW), check_vma=False)
```

profile of v0, /device:TPU:1, one launch (start us, length us, event | category | flops | bytes accessed | tf_op | source)
XLA Modules:
  0.0 70.4 jit_solution(1682825103691752986)
XLA Ops:
  0.0 0.0 copy-start
  0.0 1.6 %broadcast_in_dim.2 = bf16[8,48,512]{2,1,0:T(8,128)(2,1)} broadcast(bf16[48,512]{1,0:T(8,128)(2,1)} %param.4), dimensions={1,2} | broadcast | bytes 442368 | tf_op jit(solution)/shard_map/broadcast_in_dim | solution.py:285
  1.6 6.4 %all-to-all-start = ((bf16[8,48,512]{2,1,0:T(8,128)(2,1)}), bf16[8,48,512]{2,1,0:T(8,128)(2,1)S(1)}, u32[]{:S(2)}, u32[]{:S(2)}) async-start(bf16[8,48,512]{2,1,0:T(8,128)(2,1)} %broadcast_in_dim.2), calls=%async_computation | async-start | bytes 786432 | tf_op jit(solution)/shard_map/all_to_all | solution.py:285
  8.0 1.3 %collective-permute-start = (bf16[64,512]{1,0:T(8,128)(2,1)}, bf16[64,512]{1,0:T(8,128)(2,1)S(1)}, u32[]{:S(2)}, u32[]{:S(2)}) collective-permute-start(bf16[64,512]{1,0:T(8,128)(2,1)} %param.3), channel_id=1, source_target_pairs={{4,12},{5,13},{6,14},{7,15},{8,0},{9,1},{10,2},{11,3},{12,20},{13,... | collective-permute-start | bytes 196616 | tf_op jit(solution)/shard_map/ppermute | solution.py:255
  9.2 0.8 %constant_dynamic-update-slice_fusion.1 = bf16[128,512]{1,0:T(8,128)(2,1)S(1)} fusion(bf16[64,512]{1,0:T(8,128)(2,1)} %param.3), kind=kLoop, calls=%fused_computation.1 | loop fusion | bytes 131072
  10.1 5.1 %collective-permute-done = bf16[64,512]{1,0:T(8,128)(2,1)S(1)} collective-permute-done((bf16[64,512]{1,0:T(8,128)(2,1)}, bf16[64,512]{1,0:T(8,128)(2,1)S(1)}, u32[]{:S(2)}, u32[]{:S(2)}) %collective-permute-start) | collective-permute-done | bytes 65568 | tf_op jit(solution)/shard_map/ppermute | solution.py:255
  15.2 3.4 %collective-permute-start.3 = (bf16[128,512]{1,0:T(8,128)(2,1)S(1)}, bf16[128,512]{1,0:T(8,128)(2,1)S(1)}, u32[]{:S(2)}, u32[]{:S(2)}) collective-permute-start(bf16[128,512]{1,0:T(8,128)(2,1)S(1)} %constant_dynamic-update-slice_fusion.a), channel_id=1, source_target_pairs={{0,6},{2,0},{4,2},{6,4},{1,7},{3,1},{5,3},{7,5},{8,14},{10,8},{12,... | collective-permute-start | bytes 393224 | tf_op jit(solution)/shard_map/ppermute | solution.py:288
  18.7 2.9 %collective-permute-start.2 = (bf16[128,512]{1,0:T(8,128)(2,1)S(1)}, bf16[128,512]{1,0:T(8,128)(2,1)S(1)}, u32[]{:S(2)}, u32[]{:S(2)}) collective-permute-start(bf16[128,512]{1,0:T(8,128)(2,1)S(1)} %constant_dynamic-update-slice_fusion.a), channel_id=1, source_target_pairs={{0,4},{2,6},{4,0},{6,2},{1,5},{3,7},{5,1},{7,3},{8,12},{10,14},{12... | collective-permute-start | bytes 393224 | tf_op jit(solution)/shard_map/ppermute | solution.py:288
  21.5 0.4 collective-permute-start.1
  21.9 0.0 collective-permute-done.3.d
  21.9 7.1 %collective-permute-done.2.c = bf16[128,512]{1,0:T(8,128)(2,1)S(1)} collective-permute-done((bf16[128,512]{1,0:T(8,128)(2,1)S(1)}, bf16[128,512]{1,0:T(8,128)(2,1)S(1)}, u32[]{:S(2)}, u32[]{:S(2)}) %collective-permute-start.2) | collective-permute-done | bytes 131104 | tf_op jit(solution)/shard_map/ppermute | solution.py:288
  29.0 1.8 %collective-permute-done.1.b = bf16[128,512]{1,0:T(8,128)(2,1)S(1)} collective-permute-done((bf16[128,512]{1,0:T(8,128)(2,1)S(1)}, bf16[128,512]{1,0:T(8,128)(2,1)S(1)}, u32[]{:S(2)}, u32[]{:S(2)}) %collective-permute-start.1) | collective-permute-done | bytes 131104 | tf_op jit(solution)/shard_map/ppermute | solution.py:288
  30.8 1.8 %collective-permute-start.4 = (bf16[512,512]{1,0:T(8,128)(2,1)S(1)}, bf16[512,512]{1,0:T(8,128)(2,1)S(1)}, u32[]{:S(2)}, u32[]{:S(2)}) collective-permute-start(bf16[512,512]{1,0:T(8,128)(2,1)S(1)} %shard_map.37.mine_ref), channel_id=1, source_target_pairs={{0,1},{1,0},{2,3},{3,2},{4,5},{5,4},{6,7},{7,6},{8,9},{9,8},{10,11... | collective-permute-start | bytes 1572872 | tf_op jit(solution)/shard_map/ppermute | solution.py:290
  32.7 0.0 all-to-all-done
  32.7 7.1 %collective-permute-start.7 = (bf16[384,512]{1,0:T(8,128)(2,1)S(1)}, bf16[384,512]{1,0:T(8,128)(2,1)S(1)}, u32[]{:S(2)}, u32[]{:S(2)}) collective-permute-start(bf16[384,512]{1,0:T(8,128)(2,1)S(1)} %bitcast.8), channel_id=1, source_target_pairs={{0,48},{1,193},{2,50},{3,195},{4,52},{5,197},{6,54},{7,199},{8,56}... | collective-permute-start | bytes 1179656 | tf_op jit(solution)/shard_map/ppermute | solution.py:255
  39.8 0.8 %collective-permute-start.6 = (bf16[384,512]{1,0:T(8,128)(2,1)S(1)}, bf16[384,512]{1,0:T(8,128)(2,1)S(1)}, u32[]{:S(2)}, u32[]{:S(2)}) collective-permute-start(bf16[384,512]{1,0:T(8,128)(2,1)S(1)} %bitcast.9), channel_id=1, source_target_pairs={{0,32},{1,129},{2,34},{3,131},{4,36},{5,133},{6,38},{7,135},{8,40}... | collective-permute-start | bytes 1179656 | tf_op jit(solution)/shard_map/ppermute | solution.py:255
  40.6 0.6 collective-permute-start.5
  41.2 0.1 pad_add_fusion.place_ref
  41.3 0.1 add_convert_fusion.flag_ref
  41.3 7.4 %collective-permute-done.7.slot_d = bf16[384,512]{1,0:T(8,128)(2,1)S(1)} collective-permute-done((bf16[384,512]{1,0:T(8,128)(2,1)S(1)}, bf16[384,512]{1,0:T(8,128)(2,1)S(1)}, u32[]{:S(2)}, u32[]{:S(2)}) %collective-permute-start.7) | collective-permute-done | bytes 393248 | tf_op jit(solution)/shard_map/ppermute | solution.py:255
  48.7 0.0 collective-permute-done.6.slot_c
  48.7 3.4 %collective-permute-done.5.slot_b = bf16[384,512]{1,0:T(8,128)(2,1)S(1)} collective-permute-done((bf16[384,512]{1,0:T(8,128)(2,1)S(1)}, bf16[384,512]{1,0:T(8,128)(2,1)S(1)}, u32[]{:S(2)}, u32[]{:S(2)}) %collective-permute-start.5) | collective-permute-done | bytes 393248 | tf_op jit(solution)/shard_map/ppermute | solution.py:255
  52.1 0.7 shard_map.38
  52.8 1.9 %collective-permute-start.9 = (bf16[192,512]{1,0:T(8,128)(2,1)S(1)}, bf16[192,512]{1,0:T(8,128)(2,1)S(1)}, u32[]{:S(2)}, u32[]{:S(2)}) collective-permute-start(bf16[192,512]{1,0:T(8,128)(2,1)S(1)} %get-tuple-element.17), channel_id=1, source_target_pairs={{1,0},{2,1},{3,2},{4,3},{5,4},{6,5},{7,6},{9,8},{10,9},{11,10},{12... | collective-permute-start | bytes 589832 | tf_op jit(solution)/shard_map/ppermute | solution.py:294
  54.8 4.5 %collective-permute-start.8 = (bf16[256,512]{1,0:T(8,128)(2,1)S(1)}, bf16[256,512]{1,0:T(8,128)(2,1)S(1)}, u32[]{:S(2)}, u32[]{:S(2)}) collective-permute-start(bf16[256,512]{1,0:T(8,128)(2,1)S(1)} %get-tuple-element.16), channel_id=1, source_target_pairs={{0,1},{1,2},{2,3},{3,4},{4,5},{5,6},{6,7},{8,9},{9,10},{10,11},{11... | collective-permute-start | bytes 786440 | tf_op jit(solution)/shard_map/ppermute | solution.py:293
  59.3 0.0 collective-permute-done.4.other_ref
  59.3 0.0 copy-done
  59.3 5.0 %shard_map.39 = (bf16[1024,512]{1,0:T(8,128)(2,1)S(1)}, f32[17,4,30,8,128]{4,3,2,1,0:T(8,128)S(1)}, f32[14,512,128]{2,1,0:T(8,128)S(1)}) custom-call(bf16[512,512]{1,0:T(8,128)(2,1)S(1)} %shard_map.37.mine_ref, bf16[512,512]{1,0:T(8,128)(2,1)S(1)} %collective-permute-done.4.other_ref, bf16[1536,512]{1,0:T(8,128)(2,1)S(1)} %get-tuple-element.12.refs_ref, ...), custom_call_target="tpu_custom_call" | custom-call | flops 4294967296 | bytes 12582912 | tf_op jit(solution)/shard_map/pallas_call | solution.py:233
  64.4 0.0 collective-permute-done.9.right_ref
  64.4 0.0 collective-permute-done.8.left_ref
  64.4 6.0 %shard_map.40 = (f32[17,4,30,8,128]{4,3,2,1,0:T(8,128)S(1)}, f32[14,512,128]{2,1,0:T(8,128)S(1)}, f32[512,1536]{1,0:T(8,128)}) custom-call(f32[17,4,30,8,128]{4,3,2,1,0:T(8,128)S(1)} %get-tuple-element.13.base_in, f32[14,512,128]{2,1,0:T(8,128)S(1)} %get-tuple-element.14.res_in, ...), custom_call_target="tpu_custom_call", output_to_operand_aliasing={{0}: (0, {}), {1}: (1, {})} | custom-call | flops 4294967296 | bytes 12582912 | tf_op jit(solution)/shard_map/pallas_call | solution.py:240
  (2 shorter events, 0.0 us)
Async XLA Ops:
  0.0 59.3 %copy-start = (f32[2,8]{1,0:T(2,128)S(1)}, f32[2,8]{1,0:T(2,128)}, u32[]{:S(2)}) copy-start(f32[2,8]{1,0:T(2,128)} %taps_ref.3) | copy-start | bytes 196
  1.6 31.1 %all-to-all-start = ((bf16[8,48,512]{2,1,0:T(8,128)(2,1)}), bf16[8,48,512]{2,1,0:T(8,128)(2,1)S(1)}, u32[]{:S(2)}, u32[]{:S(2)}) async-start(bf16[8,48,512]{2,1,0:T(8,128)(2,1)} %broadcast_in_dim.2), calls=%async_computation | async-start | bytes 786432 | tf_op jit(solution)/shard_map/all_to_all | solution.py:285
  8.0 7.3 %collective-permute-start = (bf16[64,512]{1,0:T(8,128)(2,1)}, bf16[64,512]{1,0:T(8,128)(2,1)S(1)}, u32[]{:S(2)}, u32[]{:S(2)}) collective-permute-start(bf16[64,512]{1,0:T(8,128)(2,1)} %param.3), channel_id=1, source_target_pairs={{4,12},{5,13},{6,14},{7,15},{8,0},{9,1},{10,2},{11,3},{12,20},{13,... | collective-permute-start | bytes 196616 | tf_op jit(solution)/shard_map/ppermute | solution.py:255
  15.2 6.7 %collective-permute-start.3 = (bf16[128,512]{1,0:T(8,128)(2,1)S(1)}, bf16[128,512]{1,0:T(8,128)(2,1)S(1)}, u32[]{:S(2)}, u32[]{:S(2)}) collective-permute-start(bf16[128,512]{1,0:T(8,128)(2,1)S(1)} %constant_dynamic-update-slice_fusion.a), channel_id=1, source_target_pairs={{0,6},{2,0},{4,2},{6,4},{1,7},{3,1},{5,3},{7,5},{8,14},{10,8},{12,... | collective-permute-start | bytes 393224 | tf_op jit(solution)/shard_map/ppermute | solution.py:288
  18.7 10.3 %collective-permute-start.2 = (bf16[128,512]{1,0:T(8,128)(2,1)S(1)}, bf16[128,512]{1,0:T(8,128)(2,1)S(1)}, u32[]{:S(2)}, u32[]{:S(2)}) collective-permute-start(bf16[128,512]{1,0:T(8,128)(2,1)S(1)} %constant_dynamic-update-slice_fusion.a), channel_id=1, source_target_pairs={{0,4},{2,6},{4,0},{6,2},{1,5},{3,7},{5,1},{7,3},{8,12},{10,14},{12... | collective-permute-start | bytes 393224 | tf_op jit(solution)/shard_map/ppermute | solution.py:288
  21.5 9.3 %collective-permute-start.1 = (bf16[128,512]{1,0:T(8,128)(2,1)S(1)}, bf16[128,512]{1,0:T(8,128)(2,1)S(1)}, u32[]{:S(2)}, u32[]{:S(2)}) collective-permute-start(bf16[128,512]{1,0:T(8,128)(2,1)S(1)} %constant_dynamic-update-slice_fusion.a), channel_id=1, source_target_pairs={{0,2},{2,4},{4,6},{6,0},{1,3},{3,5},{5,7},{7,1},{8,10},{10,12},{12... | collective-permute-start | bytes 393224 | tf_op jit(solution)/shard_map/ppermute | solution.py:288
  30.8 28.5 %collective-permute-start.4 = (bf16[512,512]{1,0:T(8,128)(2,1)S(1)}, bf16[512,512]{1,0:T(8,128)(2,1)S(1)}, u32[]{:S(2)}, u32[]{:S(2)}) collective-permute-start(bf16[512,512]{1,0:T(8,128)(2,1)S(1)} %shard_map.37.mine_ref), channel_id=1, source_target_pairs={{0,1},{1,0},{2,3},{3,2},{4,5},{5,4},{6,7},{7,6},{8,9},{9,8},{10,11... | collective-permute-start | bytes 1572872 | tf_op jit(solution)/shard_map/ppermute | solution.py:290
  32.7 16.1 %collective-permute-start.7 = (bf16[384,512]{1,0:T(8,128)(2,1)S(1)}, bf16[384,512]{1,0:T(8,128)(2,1)S(1)}, u32[]{:S(2)}, u32[]{:S(2)}) collective-permute-start(bf16[384,512]{1,0:T(8,128)(2,1)S(1)} %bitcast.8), channel_id=1, source_target_pairs={{0,48},{1,193},{2,50},{3,195},{4,52},{5,197},{6,54},{7,199},{8,56}... | collective-permute-start | bytes 1179656 | tf_op jit(solution)/shard_map/ppermute | solution.py:255
  39.8 8.9 %collective-permute-start.6 = (bf16[384,512]{1,0:T(8,128)(2,1)S(1)}, bf16[384,512]{1,0:T(8,128)(2,1)S(1)}, u32[]{:S(2)}, u32[]{:S(2)}) collective-permute-start(bf16[384,512]{1,0:T(8,128)(2,1)S(1)} %bitcast.9), channel_id=1, source_target_pairs={{0,32},{1,129},{2,34},{3,131},{4,36},{5,133},{6,38},{7,135},{8,40}... | collective-permute-start | bytes 1179656 | tf_op jit(solution)/shard_map/ppermute | solution.py:255
  40.6 11.5 %collective-permute-start.5 = (bf16[384,512]{1,0:T(8,128)(2,1)S(1)}, bf16[384,512]{1,0:T(8,128)(2,1)S(1)}, u32[]{:S(2)}, u32[]{:S(2)}) collective-permute-start(bf16[384,512]{1,0:T(8,128)(2,1)S(1)} %bitcast.10), channel_id=1, source_target_pairs={{0,16},{1,65},{2,18},{3,67},{4,20},{5,69},{6,22},{7,71},{8,24},{9,... | collective-permute-start | bytes 1179656 | tf_op jit(solution)/shard_map/ppermute | solution.py:255
  52.8 11.5 %collective-permute-start.9 = (bf16[192,512]{1,0:T(8,128)(2,1)S(1)}, bf16[192,512]{1,0:T(8,128)(2,1)S(1)}, u32[]{:S(2)}, u32[]{:S(2)}) collective-permute-start(bf16[192,512]{1,0:T(8,128)(2,1)S(1)} %get-tuple-element.17), channel_id=1, source_target_pairs={{1,0},{2,1},{3,2},{4,3},{5,4},{6,5},{7,6},{9,8},{10,9},{11,10},{12... | collective-permute-start | bytes 589832 | tf_op jit(solution)/shard_map/ppermute | solution.py:294
  54.8 9.6 %collective-permute-start.8 = (bf16[256,512]{1,0:T(8,128)(2,1)S(1)}, bf16[256,512]{1,0:T(8,128)(2,1)S(1)}, u32[]{:S(2)}, u32[]{:S(2)}) collective-permute-start(bf16[256,512]{1,0:T(8,128)(2,1)S(1)} %get-tuple-element.16), channel_id=1, source_target_pairs={{0,1},{1,2},{2,3},{3,4},{4,5},{5,6},{6,7},{8,9},{9,10},{10,11},{11... | collective-permute-start | bytes 786440 | tf_op jit(solution)/shard_map/ppermute | solution.py:293
where the time goes:
time: 70.7 us; the launch traced here: 70.4 us
  starting transfers between devices  31.1 us (44%)
  waiting for transfers between devices  24.8 us (35%)
  Pallas kernels  11.7 us (17%)
  local copies, waits for them, and re-layouts  2.44 us (3%)
    ppermute x4, waiting for transfers between devices, move_rows(): return lax.ppermute(value, PB + ROW, pairs)  16 us
    ppermute x4, starting transfers between devices, move_rows(): return lax.ppermute(value, PB + ROW, pairs)  9.79 us
    ppermute x3, waiting for transfers between devices, local(): lax.ppermute(both, 'zh', [(i, (i + d) % 4) for i in range(4)])  8.88 us
    ppermute x3, starting transfers between devices, local(): lax.ppermute(both, 'zh', [(i, (i + d) % 4) for i in range(4)])  6.66 us
    all_to_all x1, starting transfers between devices, local(): lax.all_to_all(jnp.broadcast_to(r[None], (8, 48, DESC)), PB + ('c',), 0,...  6.36 us
    pallas_call x1, Pallas kernels, run_edges(): pl.pallas_call(edges, out_shape=[f32(*BASE), f32(*RES), f32(512, 1536)],...  5.99 us
    pallas_call x1, Pallas kernels, run_middle(): pl.pallas_call(middle, out_shape=[rows_of(1024), f32(*BASE), f32(*RES)],...  5.02 us
    ppermute x1, starting transfers between devices, local(): left = lax.ppermute(send_left, ROW, [(i, i + 1) for i in range(7)])  4.54 us
  transfers between devices with their start and end apart: 11, of which 5 were waited for; matrix products, arithmetic and copies ran while one was open for 1% of the time, Pallas kernels for 8%

commit v1 on v0

--- a/solution.py
+++ b/solution.py
@@ -128,14 +128,22 @@
     return diagonals
 
 
-def middle(mine_ref, other_ref, refs_ref, taps_ref, flag_ref, place_ref, qs, base, res):
+def middle(mine_ref, near_ref, far_ref, refs_ref, taps_ref, flag_ref, place_ref, qs, base, res):
     zh, core = place_ref[0], place_ref[1]
-    for s in range(4):
-        for ref, c in ((mine_ref, core), (other_ref, 1 - core)):
-            w = 2 * lax.rem(zh - s + 4, 4) + c
-            qs[pl.ds(pl.multiple_of(256 + w * 64, 64), 64), :] = ref[s * 128:s * 128 + 64, :]
-            rim = jnp.where(w >= 4, (w - 4) * 64, 768 + w * 64)
-            qs[pl.ds(pl.multiple_of(rim, 64), 64), :] = ref[s * 128 + 64:s * 128 + 128, :]
+
+    def put(ref, at, z, c):
+        w = 2 * lax.rem(z + 8, 4) + c
+        qs[pl.ds(pl.multiple_of(256 + w * 64, 64), 64), :] = ref[at:at + 64, :]
+        rim = jnp.where(w >= 4, (w - 4) * 64, 768 + w * 64)
+        qs[pl.ds(pl.multiple_of(rim, 64), 64), :] = ref[at + 64:at + 128, :]
+
+    put(mine_ref, 0, zh, core)
+    put(mine_ref, 128, zh, 1 - core)
+    for ref, c in ((near_ref, core), (far_ref, 1 - core)):
+        z = zh - 1 + 2 * c
+        put(ref, 0, z, c)
+        put(ref, 128, z, 1 - c)
+        put(ref, 256, zh + 2, c)
 
     def rows(start, size):
         return lambda c: refs_ref[pl.ds(pl.multiple_of(start + c * D, D), size), :]
@@ -211,15 +219,27 @@
 BASE, RES = (17, 4, NB, 8, 128), (14, 512, 128)
 
 
-def pack(a, b, c, d, stack):
-    for s, ref in enumerate((a, b, c, d)):
-        stack[s * 128:s * 128 + 128, :] = ref[...]
-
-
-def run_pack(parts):
-    return pl.pallas_call(
-        pack, out_shape=rows_of(512), in_specs=[VMEM] * 4, out_specs=VMEM,
+def pack(*refs):
+    at = 0
+    for ref in refs[:-1]:
+        refs[-1][at:at + ref.shape[0], :] = ref[...]
+        at += ref.shape[0]
+
+
+def run_pack(*parts):
+    return pl.pallas_call(
+        pack, out_shape=rows_of(sum(p.shape[0] for p in parts)), in_specs=[VMEM] * len(parts), out_specs=VMEM,
         compiler_params=params(4), cost_estimate=cost(0, 1 << 20))(*parts)
+
+
+def head(ref, out):
+    out[...] = ref[0:128, :]
+
+
+def run_head(value):
+    return pl.pallas_call(
+        head, out_shape=rows_of(128), in_specs=[VMEM], out_specs=VMEM,
+        compiler_params=params(4), cost_estimate=cost(0, 1 << 18))(value)
 
 
 def run_arrange(slots, place):
@@ -229,11 +249,11 @@
         compiler_params=params(8), cost_estimate=cost(0, 3 << 20))(*slots, place)
 
 
-def run_middle(mine, other, refs, taps, flags, place):
+def run_middle(mine, near, far, refs, taps, flags, place):
     return pl.pallas_call(
         middle, out_shape=[rows_of(1024), f32(*BASE), f32(*RES)],
-        in_specs=[VMEM] * 3 + [SMEM] * 3, out_specs=[VMEM] * 3,
-        compiler_params=params(20), cost_estimate=cost(1 << 32, 12 << 20))(mine, other, refs, taps, flags, place)
+        in_specs=[VMEM] * 4 + [SMEM] * 3, out_specs=[VMEM] * 3,
+        compiler_params=params(20), cost_estimate=cost(1 << 32, 12 << 20))(mine, near, far, refs, taps, flags, place)
 
 
 def run_edges(base, res, qs, refs, left, right, taps, flags):
@@ -268,6 +288,10 @@
     return move
 
 
+def turn(x, y, zl, zh, c):
+    return (x, y, zl, (zh + 1 - 2 * c) % 4, c)
+
+
 def first_groups():
     at = lambda *i: int(np.ravel_multi_index(i, (4, 4, 2, 2)))
     rows = [[at(x, y, z, 0) for x in range(4) for z in range(2)] for y in range(4)]
@@ -281,18 +305,21 @@
     flags = jnp.stack([pb != 0, pb != 31, row != 0, row != 7]).astype(jnp.float32)
     place = jnp.stack([index["zh"], index["c"], second])
 
-    rim = move_rows(q, rim_of_queries)
     block = lax.all_to_all(jnp.broadcast_to(r[None], (8, 48, DESC)), PB + ("c",), 0, 0,
                            axis_index_groups=first_groups(), tiled=True).reshape(384, DESC)
-    both = jnp.concatenate([q, rim], axis=0)
-    turned = [lax.ppermute(both, "zh", [(i, (i + d) % 4) for i in range(4)]) for d in (1, 2, 3)]
-    stack = run_pack([both] + turned)
-    other = lax.ppermute(stack, "c", [(0, 1), (1, 0)])
+    rim = move_rows(q, rim_of_queries)
+    both = run_pack(q, rim)
+    mine = run_pack(both, lax.ppermute(both, "c", [(0, 1), (1, 0)]))
+    near = move_rows(mine, turn)
+    part = run_head(near)
+    far = move_rows(part, turn)
+    near = run_pack(near, far)
+    far = lax.ppermute(near, "c", [(0, 1), (1, 0)])
     slots = [block] + [move_rows(block, along_second(d)) for d in (1, 2, 3)]
     refs, send_left, send_right = run_arrange(slots, place)
     left = lax.ppermute(send_left, ROW, [(i, i + 1) for i in range(7)])
     right = lax.ppermute(send_right, ROW, [(i + 1, i) for i in range(7)])
-    qs, base, res = run_middle(stack, other, refs, taps, flags, place)
+    qs, base, res = run_middle(mine, near, far, refs, taps, flags, place)
     return run_edges(base, res, qs, refs, left, right, taps, flags)
 
 

time: 70.7 us -> 69.5 us (0.983)
  starting transfers between devices: 31.1 us -> 29.9 us
    ppermute x4 -> x2, waiting for transfers between devices: 8.88 us -> 0.99 us  [the longest x1 0.99 us: local(): mine = run_pack(both, lax.ppermute(both, 'c', [(0, 1), (1, 0)]))]
    ppermute x4 -> x6, waiting for transfers between devices: 16 us -> 23.6 us  [move_rows(): return lax.ppermute(value, PB + ROW, pairs)]
    ppermute x4 -> x2, starting transfers between devices: 8.5 us -> 1.82 us  [the longest x1 1.73 us: local(): mine = run_pack(both, lax.ppermute(both, 'c', [(0, 1), (1, 0)]))]
    ppermute x4 -> x6, starting transfers between devices: 9.79 us -> 14.1 us  [move_rows(): return lax.ppermute(value, PB + ROW, pairs)]
    ppermute x1, starting transfers between devices: 4.54 us -> 5.7 us  [local(): left = lax.ppermute(send_left, ROW, [(i, i + 1) for i in range(7)])]
  transfers between devices with their start and end apart: 11 -> 11, of which waited for: 5 -> 5; matrix products, arithmetic and copies ran while one was open for 1% -> 0% of each run, Pallas kernels for 8% -> 8%
where the time goes in v1:
time: 69.5 us; the launch traced here: 69.1 us
  starting transfers between devices  29.9 us (43%)
  waiting for transfers between devices  24.6 us (35%)
  Pallas kernels  11.8 us (17%)
  local copies, waits for them, and re-layouts  2.43 us (3%)
    ppermute x6, waiting for transfers between devices, move_rows(): return lax.ppermute(value, PB + ROW, pairs)  23.6 us
    ppermute x6, starting transfers between devices, move_rows(): return lax.ppermute(value, PB + ROW, pairs)  14.1 us
    all_to_all x1, starting transfers between devices, local(): lax.all_to_all(jnp.broadcast_to(r[None], (8, 48, DESC)), PB + ('c',), 0,...  6.36 us
    pallas_call x1, Pallas kernels, run_edges(): pl.pallas_call(edges, out_shape=[f32(*BASE), f32(*RES), f32(512, 1536)],...  6.05 us
    ppermute x1, starting transfers between devices, local(): left = lax.ppermute(send_left, ROW, [(i, i + 1) for i in range(7)])  5.7 us
    pallas_call x1, Pallas kernels, run_middle(): pl.pallas_call(middle, out_shape=[rows_of(1024), f32(*BASE), f32(*RES)],...  5.05 us
    ppermute x1, starting transfers between devices, local(): right = lax.ppermute(send_right, ROW, [(i + 1, i) for i in range(7)])  1.92 us
    ppermute x1, starting transfers between devices, local(): mine = run_pack(both, lax.ppermute(both, 'c', [(0, 1), (1, 0)]))  1.73 us
  transfers between devices with their start and end apart: 11, of which 5 were waited for; matrix products, arithmetic and copies ran while one was open for 0% of the time, Pallas kernels for 8%

profile of v1, /device:TPU:1, one launch (start us, length us, event | category | flops | bytes accessed | tf_op | source)
XLA Modules:
  0.0 69.1 jit_solution(12318104676574042537)
XLA Ops:
  0.0 0.0 copy-start.1
  0.0 1.6 %broadcast_in_dim.2 = bf16[8,48,512]{2,1,0:T(8,128)(2,1)} broadcast(bf16[48,512]{1,0:T(8,128)(2,1)} %param.4), dimensions={1,2} | broadcast | bytes 442368 | tf_op jit(solution)/shard_map/broadcast_in_dim | solution.py:308
  1.6 6.4 %all-to-all-start = ((bf16[8,48,512]{2,1,0:T(8,128)(2,1)}), bf16[8,48,512]{2,1,0:T(8,128)(2,1)S(1)}, u32[]{:S(2)}, u32[]{:S(2)}) async-start(bf16[8,48,512]{2,1,0:T(8,128)(2,1)} %broadcast_in_dim.2), calls=%async_computation | async-start | bytes 786432 | tf_op jit(solution)/shard_map/all_to_all | solution.py:308
  8.0 1.3 %collective-permute-start = (bf16[64,512]{1,0:T(8,128)(2,1)}, bf16[64,512]{1,0:T(8,128)(2,1)S(1)}, u32[]{:S(2)}, u32[]{:S(2)}) collective-permute-start(bf16[64,512]{1,0:T(8,128)(2,1)} %refs_0_.1), channel_id=1, source_target_pairs={{4,12},{5,13},{6,14},{7,15},{8,0},{9,1},{10,2},{11,3},{12,20},{13,... | collective-permute-start | bytes 196616 | tf_op jit(solution)/shard_map/ppermute | solution.py:275
  9.2 6.0 %collective-permute-done.refs_1_ = bf16[64,512]{1,0:T(8,128)(2,1)S(1)} collective-permute-done((bf16[64,512]{1,0:T(8,128)(2,1)}, bf16[64,512]{1,0:T(8,128)(2,1)S(1)}, u32[]{:S(2)}, u32[]{:S(2)}) %collective-permute-start) | collective-permute-done | bytes 65568 | tf_op jit(solution)/shard_map/ppermute | solution.py:275
  15.2 0.0 copy-start
  15.2 0.8 %copy-done = bf16[64,512]{1,0:T(8,128)(2,1)S(1)} copy-done((bf16[64,512]{1,0:T(8,128)(2,1)S(1)}, bf16[64,512]{1,0:T(8,128)(2,1)}, u32[]{:S(2)}) %copy-start) | copy-done | bytes 65560
  16.1 1.7 %collective-permute-start.1 = (bf16[128,512]{1,0:T(8,128)(2,1)S(1)}, bf16[128,512]{1,0:T(8,128)(2,1)S(1)}, u32[]{:S(2)}, u32[]{:S(2)}) collective-permute-start(bf16[128,512]{1,0:T(8,128)(2,1)S(1)} %shard_map.37.refs_0_), channel_id=1, source_target_pairs={{0,1},{1,0},{2,3},{3,2},{4,5},{5,4},{6,7},{7,6},{8,9},{9,8},{10,11... | collective-permute-start | bytes 393224 | tf_op jit(solution)/shard_map/ppermute | solution.py:312
  17.8 1.0 %collective-permute-done.1.refs_1_ = bf16[128,512]{1,0:T(8,128)(2,1)S(1)} collective-permute-done((bf16[128,512]{1,0:T(8,128)(2,1)S(1)}, bf16[128,512]{1,0:T(8,128)(2,1)S(1)}, u32[]{:S(2)}, u32[]{:S(2)}) %collective-permute-start.1) | collective-permute-done | bytes 131104 | tf_op jit(solution)/shard_map/ppermute | solution.py:312
  18.8 3.2 %collective-permute-start.2 = (bf16[256,512]{1,0:T(8,128)(2,1)S(1)}, bf16[256,512]{1,0:T(8,128)(2,1)S(1)}, u32[]{:S(2)}, u32[]{:S(2)}) collective-permute-start(bf16[256,512]{1,0:T(8,128)(2,1)S(1)} %shard_map.38.mine_ref), channel_id=1, source_target_pairs={{0,2},{1,7},{2,4},{3,1},{4,6},{5,3},{6,0},{7,5},{8,10},{9,15},{10,... | collective-permute-start | bytes 786440 | tf_op jit(solution)/shard_map/ppermute | solution.py:275
  22.0 6.5 %collective-permute-done.2.ref.refs_0_ = bf16[256,512]{1,0:T(8,128)(2,1)S(1)} collective-permute-done((bf16[256,512]{1,0:T(8,128)(2,1)S(1)}, bf16[256,512]{1,0:T(8,128)(2,1)S(1)}, u32[]{:S(2)}, u32[]{:S(2)}) %collective-permute-start.2) | collective-permute-done | bytes 262176 | tf_op jit(solution)/shard_map/ppermute | solution.py:275
  28.5 2.4 %collective-permute-start.3 = (bf16[128,512]{1,0:T(8,128)(2,1)S(1)}, bf16[128,512]{1,0:T(8,128)(2,1)S(1)}, u32[]{:S(2)}, u32[]{:S(2)}) collective-permute-start(bf16[128,512]{1,0:T(8,128)(2,1)S(1)} %shard_map.39), channel_id=1, source_target_pairs={{0,2},{1,7},{2,4},{3,1},{4,6},{5,3},{6,0},{7,5},{8,10},{9,15},{10,... | collective-permute-start | bytes 393224 | tf_op jit(solution)/shard_map/ppermute | solution.py:275
  30.9 0.0 all-to-all-done
  30.9 6.4 %collective-permute-start.7 = (bf16[384,512]{1,0:T(8,128)(2,1)S(1)}, bf16[384,512]{1,0:T(8,128)(2,1)S(1)}, u32[]{:S(2)}, u32[]{:S(2)}) collective-permute-start(bf16[384,512]{1,0:T(8,128)(2,1)S(1)} %bitcast.8), channel_id=1, source_target_pairs={{0,48},{1,193},{2,50},{3,195},{4,52},{5,197},{6,54},{7,199},{8,56}... | collective-permute-start | bytes 1179656 | tf_op jit(solution)/shard_map/ppermute | solution.py:275
  37.3 0.3 collective-permute-start.6
  37.6 0.6 collective-permute-start.5
  38.2 0.0 collective-permute-done.3.refs_1_
  38.2 0.1 collective-permute-start.4
  38.3 0.1 pad_add_fusion.place_ref
  38.4 0.1 add_convert_fusion.flag_ref
  38.5 7.8 %collective-permute-done.7.slot_d = bf16[384,512]{1,0:T(8,128)(2,1)S(1)} collective-permute-done((bf16[384,512]{1,0:T(8,128)(2,1)S(1)}, bf16[384,512]{1,0:T(8,128)(2,1)S(1)}, u32[]{:S(2)}, u32[]{:S(2)}) %collective-permute-start.7) | collective-permute-done | bytes 393248 | tf_op jit(solution)/shard_map/ppermute | solution.py:275
  46.3 0.0 collective-permute-done.6.slot_c
  46.3 3.4 %collective-permute-done.5.slot_b = bf16[384,512]{1,0:T(8,128)(2,1)S(1)} collective-permute-done((bf16[384,512]{1,0:T(8,128)(2,1)S(1)}, bf16[384,512]{1,0:T(8,128)(2,1)S(1)}, u32[]{:S(2)}, u32[]{:S(2)}) %collective-permute-start.5) | collective-permute-done | bytes 393248 | tf_op jit(solution)/shard_map/ppermute | solution.py:275
  49.7 0.7 shard_map.41
  50.3 1.9 %collective-permute-start.9 = (bf16[192,512]{1,0:T(8,128)(2,1)S(1)}, bf16[192,512]{1,0:T(8,128)(2,1)S(1)}, u32[]{:S(2)}, u32[]{:S(2)}) collective-permute-start(bf16[192,512]{1,0:T(8,128)(2,1)S(1)} %get-tuple-element.17), channel_id=1, source_target_pairs={{1,0},{2,1},{3,2},{4,3},{5,4},{6,5},{7,6},{9,8},{10,9},{11,10},{12... | collective-permute-start | bytes 589832 | tf_op jit(solution)/shard_map/ppermute | solution.py:321
  52.3 5.7 %collective-permute-start.8 = (bf16[256,512]{1,0:T(8,128)(2,1)S(1)}, bf16[256,512]{1,0:T(8,128)(2,1)S(1)}, u32[]{:S(2)}, u32[]{:S(2)}) collective-permute-start(bf16[256,512]{1,0:T(8,128)(2,1)S(1)} %get-tuple-element.16), channel_id=1, source_target_pairs={{0,1},{1,2},{2,3},{3,4},{4,5},{5,6},{6,7},{8,9},{9,10},{10,11},{11... | collective-permute-start | bytes 786440 | tf_op jit(solution)/shard_map/ppermute | solution.py:320
  58.0 0.0 collective-permute-done.4.far_ref
  58.0 0.0 copy-done.1
  58.0 5.0 %shard_map.42 = (bf16[1024,512]{1,0:T(8,128)(2,1)S(1)}, f32[17,4,30,8,128]{4,3,2,1,0:T(8,128)S(1)}, f32[14,512,128]{2,1,0:T(8,128)S(1)}) custom-call(bf16[256,512]{1,0:T(8,128)(2,1)S(1)} %shard_map.38.mine_ref, bf16[384,512]{1,0:T(8,128)(2,1)S(1)} %shard_map.40.near_ref, bf16[384,512]{1,0:T(8,128)(2,1)S(1)} %collective-permute-done.4.far_ref, ...), custom_call_target="tpu_custom_call" | custom-call | flops 4294967296 | bytes 12582912 | tf_op jit(solution)/shard_map/pallas_call | solution.py:253
  63.0 0.0 collective-permute-done.9.right_ref
  63.0 0.0 collective-permute-done.8.left_ref
  63.1 6.0 %shard_map.43 = (f32[17,4,30,8,128]{4,3,2,1,0:T(8,128)S(1)}, f32[14,512,128]{2,1,0:T(8,128)S(1)}, f32[512,1536]{1,0:T(8,128)}) custom-call(f32[17,4,30,8,128]{4,3,2,1,0:T(8,128)S(1)} %get-tuple-element.13.base_in, f32[14,512,128]{2,1,0:T(8,128)S(1)} %get-tuple-element.14.res_in, ...), custom_call_target="tpu_custom_call", output_to_operand_aliasing={{0}: (0, {}), {1}: (1, {})} | custom-call | flops 4294967296 | bytes 12582912 | tf_op jit(solution)/shard_map/pallas_call | solution.py:260
  (4 shorter events, 0.1 us)
Async XLA Ops:
  0.0 58.0 %copy-start.1 = (f32[2,8]{1,0:T(2,128)S(1)}, f32[2,8]{1,0:T(2,128)}, u32[]{:S(2)}) copy-start(f32[2,8]{1,0:T(2,128)} %taps_ref.3) | copy-start | bytes 196
  1.6 29.3 %all-to-all-start = ((bf16[8,48,512]{2,1,0:T(8,128)(2,1)}), bf16[8,48,512]{2,1,0:T(8,128)(2,1)S(1)}, u32[]{:S(2)}, u32[]{:S(2)}) async-start(bf16[8,48,512]{2,1,0:T(8,128)(2,1)} %broadcast_in_dim.2), calls=%async_computation | async-start | bytes 786432 | tf_op jit(solution)/shard_map/all_to_all | solution.py:308
  8.0 7.3 %collective-permute-start = (bf16[64,512]{1,0:T(8,128)(2,1)}, bf16[64,512]{1,0:T(8,128)(2,1)S(1)}, u32[]{:S(2)}, u32[]{:S(2)}) collective-permute-start(bf16[64,512]{1,0:T(8,128)(2,1)} %refs_0_.1), channel_id=1, source_target_pairs={{4,12},{5,13},{6,14},{7,15},{8,0},{9,1},{10,2},{11,3},{12,20},{13,... | collective-permute-start | bytes 196616 | tf_op jit(solution)/shard_map/ppermute | solution.py:275
  15.2 0.8 %copy-start = (bf16[64,512]{1,0:T(8,128)(2,1)S(1)}, bf16[64,512]{1,0:T(8,128)(2,1)}, u32[]{:S(2)}) copy-start(bf16[64,512]{1,0:T(8,128)(2,1)} %refs_0_.1) | copy-start | bytes 196612
  16.1 2.7 %collective-permute-start.1 = (bf16[128,512]{1,0:T(8,128)(2,1)S(1)}, bf16[128,512]{1,0:T(8,128)(2,1)S(1)}, u32[]{:S(2)}, u32[]{:S(2)}) collective-permute-start(bf16[128,512]{1,0:T(8,128)(2,1)S(1)} %shard_map.37.refs_0_), channel_id=1, source_target_pairs={{0,1},{1,0},{2,3},{3,2},{4,5},{5,4},{6,7},{7,6},{8,9},{9,8},{10,11... | collective-permute-start | bytes 393224 | tf_op jit(solution)/shard_map/ppermute | solution.py:312
  18.8 9.7 %collective-permute-start.2 = (bf16[256,512]{1,0:T(8,128)(2,1)S(1)}, bf16[256,512]{1,0:T(8,128)(2,1)S(1)}, u32[]{:S(2)}, u32[]{:S(2)}) collective-permute-start(bf16[256,512]{1,0:T(8,128)(2,1)S(1)} %shard_map.38.mine_ref), channel_id=1, source_target_pairs={{0,2},{1,7},{2,4},{3,1},{4,6},{5,3},{6,0},{7,5},{8,10},{9,15},{10,... | collective-permute-start | bytes 786440 | tf_op jit(solution)/shard_map/ppermute | solution.py:275
  28.5 9.7 %collective-permute-start.3 = (bf16[128,512]{1,0:T(8,128)(2,1)S(1)}, bf16[128,512]{1,0:T(8,128)(2,1)S(1)}, u32[]{:S(2)}, u32[]{:S(2)}) collective-permute-start(bf16[128,512]{1,0:T(8,128)(2,1)S(1)} %shard_map.39), channel_id=1, source_target_pairs={{0,2},{1,7},{2,4},{3,1},{4,6},{5,3},{6,0},{7,5},{8,10},{9,15},{10,... | collective-permute-start | bytes 393224 | tf_op jit(solution)/shard_map/ppermute | solution.py:275
  30.9 15.4 %collective-permute-start.7 = (bf16[384,512]{1,0:T(8,128)(2,1)S(1)}, bf16[384,512]{1,0:T(8,128)(2,1)S(1)}, u32[]{:S(2)}, u32[]{:S(2)}) collective-permute-start(bf16[384,512]{1,0:T(8,128)(2,1)S(1)} %bitcast.8), channel_id=1, source_target_pairs={{0,48},{1,193},{2,50},{3,195},{4,52},{5,197},{6,54},{7,199},{8,56}... | collective-permute-start | bytes 1179656 | tf_op jit(solution)/shard_map/ppermute | solution.py:275
  37.3 8.9 %collective-permute-start.6 = (bf16[384,512]{1,0:T(8,128)(2,1)S(1)}, bf16[384,512]{1,0:T(8,128)(2,1)S(1)}, u32[]{:S(2)}, u32[]{:S(2)}) collective-permute-start(bf16[384,512]{1,0:T(8,128)(2,1)S(1)} %bitcast.9), channel_id=1, source_target_pairs={{0,32},{1,129},{2,34},{3,131},{4,36},{5,133},{6,38},{7,135},{8,40}... | collective-permute-start | bytes 1179656 | tf_op jit(solution)/shard_map/ppermute | solution.py:275
  37.6 12.1 %collective-permute-start.5 = (bf16[384,512]{1,0:T(8,128)(2,1)S(1)}, bf16[384,512]{1,0:T(8,128)(2,1)S(1)}, u32[]{:S(2)}, u32[]{:S(2)}) collective-permute-start(bf16[384,512]{1,0:T(8,128)(2,1)S(1)} %bitcast.10), channel_id=1, source_target_pairs={{0,16},{1,65},{2,18},{3,67},{4,20},{5,69},{6,22},{7,71},{8,24},{9,... | collective-permute-start | bytes 1179656 | tf_op jit(solution)/shard_map/ppermute | solution.py:275
  38.2 19.8 %collective-permute-start.4 = (bf16[384,512]{1,0:T(8,128)(2,1)S(1)}, bf16[384,512]{1,0:T(8,128)(2,1)S(1)}, u32[]{:S(2)}, u32[]{:S(2)}) collective-permute-start(bf16[384,512]{1,0:T(8,128)(2,1)S(1)} %shard_map.40.near_ref), channel_id=1, source_target_pairs={{0,1},{1,0},{2,3},{3,2},{4,5},{5,4},{6,7},{7,6},{8,9},{9,8},{10,11... | collective-permute-start | bytes 1179656 | tf_op jit(solution)/shard_map/ppermute | solution.py:317
  50.3 12.7 %collective-permute-start.9 = (bf16[192,512]{1,0:T(8,128)(2,1)S(1)}, bf16[192,512]{1,0:T(8,128)(2,1)S(1)}, u32[]{:S(2)}, u32[]{:S(2)}) collective-permute-start(bf16[192,512]{1,0:T(8,128)(2,1)S(1)} %get-tuple-element.17), channel_id=1, source_target_pairs={{1,0},{2,1},{3,2},{4,3},{5,4},{6,5},{7,6},{9,8},{10,9},{11,10},{12... | collective-permute-start | bytes 589832 | tf_op jit(solution)/shard_map/ppermute | solution.py:321
  52.3 10.8 %collective-permute-start.8 = (bf16[256,512]{1,0:T(8,128)(2,1)S(1)}, bf16[256,512]{1,0:T(8,128)(2,1)S(1)}, u32[]{:S(2)}, u32[]{:S(2)}) collective-permute-start(bf16[256,512]{1,0:T(8,128)(2,1)S(1)} %get-tuple-element.16), channel_id=1, source_target_pairs={{0,1},{1,2},{2,3},{3,4},{4,5},{5,6},{6,7},{8,9},{9,10},{10,11},{11... | collective-permute-start | bytes 786440 | tf_op jit(solution)/shard_map/ppermute | solution.py:320

commit v2 on v1

--- a/solution.py
+++ b/solution.py
@@ -128,7 +128,7 @@
     return diagonals
 
 
-def middle(mine_ref, near_ref, far_ref, refs_ref, taps_ref, flag_ref, place_ref, qs, base, res):
+def middle(both_ref, other_ref, near_ref, far_ref, refs_ref, taps_ref, flag_ref, place_ref, qs, base, res):
     zh, core = place_ref[0], place_ref[1]
 
     def put(ref, at, z, c):
@@ -137,8 +137,8 @@
         rim = jnp.where(w >= 4, (w - 4) * 64, 768 + w * 64)
         qs[pl.ds(pl.multiple_of(rim, 64), 64), :] = ref[at + 64:at + 128, :]
 
-    put(mine_ref, 0, zh, core)
-    put(mine_ref, 128, zh, 1 - core)
+    put(both_ref, 0, zh, core)
+    put(other_ref, 0, zh, 1 - core)
     for ref, c in ((near_ref, core), (far_ref, 1 - core)):
         z = zh - 1 + 2 * c
         put(ref, 0, z, c)
@@ -232,16 +232,6 @@
         compiler_params=params(4), cost_estimate=cost(0, 1 << 20))(*parts)
 
 
-def head(ref, out):
-    out[...] = ref[0:128, :]
-
-
-def run_head(value):
-    return pl.pallas_call(
-        head, out_shape=rows_of(128), in_specs=[VMEM], out_specs=VMEM,
-        compiler_params=params(4), cost_estimate=cost(0, 1 << 18))(value)
-
-
 def run_arrange(slots, place):
     return pl.pallas_call(
         arrange, out_shape=[rows_of(1536), rows_of(256), rows_of(192)],
@@ -249,11 +239,11 @@
         compiler_params=params(8), cost_estimate=cost(0, 3 << 20))(*slots, place)
 
 
-def run_middle(mine, near, far, refs, taps, flags, place):
+def run_middle(both, other, near, far, refs, taps, flags, place):
     return pl.pallas_call(
         middle, out_shape=[rows_of(1024), f32(*BASE), f32(*RES)],
-        in_specs=[VMEM] * 4 + [SMEM] * 3, out_specs=[VMEM] * 3,
-        compiler_params=params(20), cost_estimate=cost(1 << 32, 12 << 20))(mine, near, far, refs, taps, flags, place)
+        in_specs=[VMEM] * 5 + [SMEM] * 3, out_specs=[VMEM] * 3,
+        compiler_params=params(20), cost_estimate=cost(1 << 32, 12 << 20))(both, other, near, far, refs, taps, flags, place)
 
 
 def run_edges(base, res, qs, refs, left, right, taps, flags):
@@ -305,21 +295,21 @@
     flags = jnp.stack([pb != 0, pb != 31, row != 0, row != 7]).astype(jnp.float32)
     place = jnp.stack([index["zh"], index["c"], second])
 
+    rim = move_rows(q, rim_of_queries)
     block = lax.all_to_all(jnp.broadcast_to(r[None], (8, 48, DESC)), PB + ("c",), 0, 0,
                            axis_index_groups=first_groups(), tiled=True).reshape(384, DESC)
-    rim = move_rows(q, rim_of_queries)
     both = run_pack(q, rim)
-    mine = run_pack(both, lax.ppermute(both, "c", [(0, 1), (1, 0)]))
-    near = move_rows(mine, turn)
-    part = run_head(near)
-    far = move_rows(part, turn)
-    near = run_pack(near, far)
+    near = move_rows(both, turn)
+    other = lax.ppermute(both, "c", [(0, 1), (1, 0)])
+    rest = move_rows(other, turn)
+    far = move_rows(near, turn)
+    near = run_pack(near, rest, far)
     far = lax.ppermute(near, "c", [(0, 1), (1, 0)])
     slots = [block] + [move_rows(block, along_second(d)) for d in (1, 2, 3)]
     refs, send_left, send_right = run_arrange(slots, place)
     left = lax.ppermute(send_left, ROW, [(i, i + 1) for i in range(7)])
     right = lax.ppermute(send_right, ROW, [(i + 1, i) for i in range(7)])
-    qs, base, res = run_middle(mine, near, far, refs, taps, flags, place)
+    qs, base, res = run_middle(both, other, near, far, refs, taps, flags, place)
     return run_edges(base, res, qs, refs, left, right, taps, flags)
 
 

time: 69.5 us -> 65.4 us (0.941)
  waiting for transfers between devices: 24.6 us -> 13.5 us
  starting transfers between devices: 29.9 us -> 37.1 us
    ppermute x6 -> x7, waiting for transfers between devices: 23.6 us -> 13.5 us  [move_rows(): return lax.ppermute(value, PB + ROW, pairs)]
    ppermute x1, starting transfers between devices: 1.92 us -> 7.01 us  [local(): right = lax.ppermute(send_right, ROW, [(i + 1, i) for i in range(7)])]
    ppermute x1, starting transfers between devices: 0.09 us -> 4.3 us  [local(): far = lax.ppermute(near, 'c', [(0, 1), (1, 0)])]
    ppermute x1, starting transfers between devices: 5.7 us -> 1.92 us  [local(): left = lax.ppermute(send_left, ROW, [(i, i + 1) for i in range(7)])]
    ppermute x6 -> x7, starting transfers between devices: 14.1 us -> 16 us  [move_rows(): return lax.ppermute(value, PB + ROW, pairs)]
    ppermute x1, waiting for transfers between devices: 0.99 us -> 0.01 us  [local(): other = lax.ppermute(both, 'c', [(0, 1), (1, 0)])]
  transfers between devices with their start and end apart: 11 -> 12, of which waited for: 5 -> 4; matrix products, arithmetic and copies ran while one was open for 0% -> 0% of each run, Pallas kernels for 8% -> 9%
where the time goes in v2:
time: 65.4 us; the launch traced here: 65 us
  starting transfers between devices  37.1 us (57%)
  waiting for transfers between devices  13.5 us (21%)
  Pallas kernels  11.7 us (18%)
  local copies, waits for them, and re-layouts  2.43 us (4%)
    ppermute x7, starting transfers between devices, move_rows(): return lax.ppermute(value, PB + ROW, pairs)  16 us
    ppermute x7, waiting for transfers between devices, move_rows(): return lax.ppermute(value, PB + ROW, pairs)  13.5 us
    ppermute x1, starting transfers between devices, local(): right = lax.ppermute(send_right, ROW, [(i + 1, i) for i in range(7)])  7.01 us
    all_to_all x1, starting transfers between devices, local(): lax.all_to_all(jnp.broadcast_to(r[None], (8, 48, DESC)), PB + ('c',), 0,...  6.36 us
    pallas_call x1, Pallas kernels, run_edges(): pl.pallas_call(edges, out_shape=[f32(*BASE), f32(*RES), f32(512, 1536)],...  5.99 us
    pallas_call x1, Pallas kernels, run_middle(): pl.pallas_call(middle, out_shape=[rows_of(1024), f32(*BASE), f32(*RES)],...  5.02 us
    ppermute x1, starting transfers between devices, local(): far = lax.ppermute(near, 'c', [(0, 1), (1, 0)])  4.3 us
    ppermute x1, starting transfers between devices, local(): left = lax.ppermute(send_left, ROW, [(i, i + 1) for i in range(7)])  1.92 us
  transfers between devices with their start and end apart: 12, of which 4 were waited for; matrix products, arithmetic and copies ran while one was open for 0% of the time, Pallas kernels for 9%

profile of v2, /device:TPU:1, one launch (start us, length us, event | category | flops | bytes accessed | tf_op | source)
XLA Modules:
  0.0 65.0 jit_solution(8370813460718953673)
XLA Ops:
  0.0 1.6 %broadcast_in_dim.2 = bf16[8,48,512]{2,1,0:T(8,128)(2,1)} broadcast(bf16[48,512]{1,0:T(8,128)(2,1)} %param.4), dimensions={1,2} | broadcast | bytes 442368 | tf_op jit(solution)/shard_map/broadcast_in_dim | solution.py:299
  1.6 6.4 %all-to-all-start = ((bf16[8,48,512]{2,1,0:T(8,128)(2,1)}), bf16[8,48,512]{2,1,0:T(8,128)(2,1)S(1)}, u32[]{:S(2)}, u32[]{:S(2)}) async-start(bf16[8,48,512]{2,1,0:T(8,128)(2,1)} %broadcast_in_dim.2), calls=%async_computation | async-start | bytes 786432 | tf_op jit(solution)/shard_map/all_to_all | solution.py:299
  8.0 1.3 %collective-permute-start = (bf16[64,512]{1,0:T(8,128)(2,1)}, bf16[64,512]{1,0:T(8,128)(2,1)S(1)}, u32[]{:S(2)}, u32[]{:S(2)}) collective-permute-start(bf16[64,512]{1,0:T(8,128)(2,1)} %refs_0_.1), channel_id=1, source_target_pairs={{4,12},{5,13},{6,14},{7,15},{8,0},{9,1},{10,2},{11,3},{12,20},{13,... | collective-permute-start | bytes 196616 | tf_op jit(solution)/shard_map/ppermute | solution.py:265
  9.2 6.0 %collective-permute-done.refs_1_ = bf16[64,512]{1,0:T(8,128)(2,1)S(1)} collective-permute-done((bf16[64,512]{1,0:T(8,128)(2,1)}, bf16[64,512]{1,0:T(8,128)(2,1)S(1)}, u32[]{:S(2)}, u32[]{:S(2)}) %collective-permute-start) | collective-permute-done | bytes 65568 | tf_op jit(solution)/shard_map/ppermute | solution.py:265
  15.2 0.8 %copy-done = bf16[64,512]{1,0:T(8,128)(2,1)S(1)} copy-done((bf16[64,512]{1,0:T(8,128)(2,1)S(1)}, bf16[64,512]{1,0:T(8,128)(2,1)}, u32[]{:S(2)}) %copy-start) | copy-done | bytes 65560
  16.1 3.5 %collective-permute-start.2 = (bf16[128,512]{1,0:T(8,128)(2,1)S(1)}, bf16[128,512]{1,0:T(8,128)(2,1)S(1)}, u32[]{:S(2)}, u32[]{:S(2)}) collective-permute-start(bf16[128,512]{1,0:T(8,128)(2,1)S(1)} %shard_map.37.both_ref), channel_id=1, source_target_pairs={{0,2},{1,7},{2,4},{3,1},{4,6},{5,3},{6,0},{7,5},{8,10},{9,15},{10,... | collective-permute-start | bytes 393224 | tf_op jit(solution)/shard_map/ppermute | solution.py:265
  19.6 1.5 %collective-permute-start.1 = (bf16[128,512]{1,0:T(8,128)(2,1)S(1)}, bf16[128,512]{1,0:T(8,128)(2,1)S(1)}, u32[]{:S(2)}, u32[]{:S(2)}) collective-permute-start(bf16[128,512]{1,0:T(8,128)(2,1)S(1)} %shard_map.37.both_ref), channel_id=1, source_target_pairs={{0,1},{1,0},{2,3},{3,2},{4,5},{5,4},{6,7},{7,6},{8,9},{9,8},{10,11... | collective-permute-start | bytes 393224 | tf_op jit(solution)/shard_map/ppermute | solution.py:303
  21.1 0.4 collective-permute-done.2.refs_0_
  21.5 4.1 %collective-permute-start.4 = (bf16[128,512]{1,0:T(8,128)(2,1)S(1)}, bf16[128,512]{1,0:T(8,128)(2,1)S(1)}, u32[]{:S(2)}, u32[]{:S(2)}) collective-permute-start(bf16[128,512]{1,0:T(8,128)(2,1)S(1)} %collective-permute-done.2.refs_0_), channel_id=1, source_target_pairs={{0,2},{1,7},{2,4},{3,1},{4,6},{5,3},{6,0},{7,5},{8,10},{9,15},{10,... | collective-permute-start | bytes 393224 | tf_op jit(solution)/shard_map/ppermute | solution.py:265
  25.6 0.0 collective-permute-done.1.other_ref
  25.6 0.0 collective-permute-start.3
  25.6 0.0 all-to-all-done
  25.6 6.1 %collective-permute-start.8 = (bf16[384,512]{1,0:T(8,128)(2,1)S(1)}, bf16[384,512]{1,0:T(8,128)(2,1)S(1)}, u32[]{:S(2)}, u32[]{:S(2)}) collective-permute-start(bf16[384,512]{1,0:T(8,128)(2,1)S(1)} %bitcast.8), channel_id=1, source_target_pairs={{0,48},{1,193},{2,50},{3,195},{4,52},{5,197},{6,54},{7,199},{8,56}... | collective-permute-start | bytes 1179656 | tf_op jit(solution)/shard_map/ppermute | solution.py:265
  31.7 0.5 collective-permute-start.7
  32.2 0.6 collective-permute-start.6
  32.8 0.0 collective-permute-done.4.refs_2_
  32.8 0.0 collective-permute-done.3.refs_1_
  32.8 4.3 %collective-permute-start.5 = (bf16[384,512]{1,0:T(8,128)(2,1)S(1)}, bf16[384,512]{1,0:T(8,128)(2,1)S(1)}, u32[]{:S(2)}, u32[]{:S(2)}) collective-permute-start(bf16[384,512]{1,0:T(8,128)(2,1)S(1)} %shard_map.38.near_ref), channel_id=1, source_target_pairs={{0,1},{1,0},{2,3},{3,2},{4,5},{5,4},{6,7},{7,6},{8,9},{9,8},{10,11... | collective-permute-start | bytes 1179656 | tf_op jit(solution)/shard_map/ppermute | solution.py:307
  37.1 0.1 pad_add_fusion.place_ref
  37.2 0.1 add_convert_fusion.flag_ref
  37.3 3.4 %collective-permute-done.8.slot_d = bf16[384,512]{1,0:T(8,128)(2,1)S(1)} collective-permute-done((bf16[384,512]{1,0:T(8,128)(2,1)S(1)}, bf16[384,512]{1,0:T(8,128)(2,1)S(1)}, u32[]{:S(2)}, u32[]{:S(2)}) %collective-permute-start.8) | collective-permute-done | bytes 393248 | tf_op jit(solution)/shard_map/ppermute | solution.py:265
  40.6 0.0 collective-permute-done.7.slot_c
  40.6 3.7 %collective-permute-done.6.slot_b = bf16[384,512]{1,0:T(8,128)(2,1)S(1)} collective-permute-done((bf16[384,512]{1,0:T(8,128)(2,1)S(1)}, bf16[384,512]{1,0:T(8,128)(2,1)S(1)}, u32[]{:S(2)}, u32[]{:S(2)}) %collective-permute-start.6) | collective-permute-done | bytes 393248 | tf_op jit(solution)/shard_map/ppermute | solution.py:265
  44.3 0.7 %shard_map.39 = (bf16[1536,512]{1,0:T(8,128)(2,1)S(1)}, bf16[256,512]{1,0:T(8,128)(2,1)S(1)}, bf16[192,512]{1,0:T(8,128)(2,1)S(1)}) custom-call(bf16[384,512]{1,0:T(8,128)(2,1)S(1)} %bitcast.11, bf16[384,512]{1,0:T(8,128)(2,1)S(1)} %collective-permute-done.6.slot_b, bf16[384,512]{1,0:T(8,128)(2,1)S(1)} %collective-permute-done.7.slot_c, ...), custom_call_target="tpu_custom_call" | custom-call | bytes 3145728 | tf_op jit(solution)/shard_map/pallas_call | solution.py:236
  45.0 7.0 %collective-permute-start.10 = (bf16[192,512]{1,0:T(8,128)(2,1)S(1)}, bf16[192,512]{1,0:T(8,128)(2,1)S(1)}, u32[]{:S(2)}, u32[]{:S(2)}) collective-permute-start(bf16[192,512]{1,0:T(8,128)(2,1)S(1)} %get-tuple-element.17), channel_id=1, source_target_pairs={{1,0},{2,1},{3,2},{4,3},{5,4},{6,5},{7,6},{9,8},{10,9},{11,10},{12... | collective-permute-start | bytes 589832 | tf_op jit(solution)/shard_map/ppermute | solution.py:311
  52.0 1.9 %collective-permute-start.9 = (bf16[256,512]{1,0:T(8,128)(2,1)S(1)}, bf16[256,512]{1,0:T(8,128)(2,1)S(1)}, u32[]{:S(2)}, u32[]{:S(2)}) collective-permute-start(bf16[256,512]{1,0:T(8,128)(2,1)S(1)} %get-tuple-element.16), channel_id=1, source_target_pairs={{0,1},{1,2},{2,3},{3,4},{4,5},{5,6},{6,7},{8,9},{9,10},{10,11},{11... | collective-permute-start | bytes 786440 | tf_op jit(solution)/shard_map/ppermute | solution.py:310
  54.0 0.0 collective-permute-done.5.far_ref
  54.0 0.0 copy-done.1
  54.0 5.0 %shard_map.40 = (bf16[1024,512]{1,0:T(8,128)(2,1)S(1)}, f32[17,4,30,8,128]{4,3,2,1,0:T(8,128)S(1)}, f32[14,512,128]{2,1,0:T(8,128)S(1)}) custom-call(bf16[128,512]{1,0:T(8,128)(2,1)S(1)} %shard_map.37.both_ref, bf16[128,512]{1,0:T(8,128)(2,1)S(1)} %collective-permute-done.1.other_ref, bf16[384,512]{1,0:T(8,128)(2,1)S(1)} %shard_map.38.near_ref, ...), custom_call_target="tpu_custom_call" | custom-call | flops 4294967296 | bytes 12582912 | tf_op jit(solution)/shard_map/pallas_call | solution.py:243
  59.0 0.0 collective-permute-done.10.right_ref
  59.0 0.0 collective-permute-done.9.left_ref
  59.0 6.0 %shard_map.41 = (f32[17,4,30,8,128]{4,3,2,1,0:T(8,128)S(1)}, f32[14,512,128]{2,1,0:T(8,128)S(1)}, f32[512,1536]{1,0:T(8,128)}) custom-call(f32[17,4,30,8,128]{4,3,2,1,0:T(8,128)S(1)} %get-tuple-element.13.base_in, f32[14,512,128]{2,1,0:T(8,128)S(1)} %get-tuple-element.14.res_in, ...), custom_call_target="tpu_custom_call", output_to_operand_aliasing={{0}: (0, {}), {1}: (1, {})} | custom-call | flops 4294967296 | bytes 12582912 | tf_op jit(solution)/shard_map/pallas_call | solution.py:250
  (4 shorter events, 0.0 us)
Async XLA Ops:
  0.0 54.0 %copy-start.1 = (f32[2,8]{1,0:T(2,128)S(1)}, f32[2,8]{1,0:T(2,128)}, u32[]{:S(2)}) copy-start(f32[2,8]{1,0:T(2,128)} %taps_ref.3) | copy-start | bytes 196
  1.6 24.0 %all-to-all-start = ((bf16[8,48,512]{2,1,0:T(8,128)(2,1)}), bf16[8,48,512]{2,1,0:T(8,128)(2,1)S(1)}, u32[]{:S(2)}, u32[]{:S(2)}) async-start(bf16[8,48,512]{2,1,0:T(8,128)(2,1)} %broadcast_in_dim.2), calls=%async_computation | async-start | bytes 786432 | tf_op jit(solution)/shard_map/all_to_all | solution.py:299
  8.0 7.3 %collective-permute-start = (bf16[64,512]{1,0:T(8,128)(2,1)}, bf16[64,512]{1,0:T(8,128)(2,1)S(1)}, u32[]{:S(2)}, u32[]{:S(2)}) collective-permute-start(bf16[64,512]{1,0:T(8,128)(2,1)} %refs_0_.1), channel_id=1, source_target_pairs={{4,12},{5,13},{6,14},{7,15},{8,0},{9,1},{10,2},{11,3},{12,20},{13,... | collective-permute-start | bytes 196616 | tf_op jit(solution)/shard_map/ppermute | solution.py:265
  15.2 0.8 %copy-start = (bf16[64,512]{1,0:T(8,128)(2,1)S(1)}, bf16[64,512]{1,0:T(8,128)(2,1)}, u32[]{:S(2)}) copy-start(bf16[64,512]{1,0:T(8,128)(2,1)} %refs_0_.1) | copy-start | bytes 196612
  16.1 5.4 %collective-permute-start.2 = (bf16[128,512]{1,0:T(8,128)(2,1)S(1)}, bf16[128,512]{1,0:T(8,128)(2,1)S(1)}, u32[]{:S(2)}, u32[]{:S(2)}) collective-permute-start(bf16[128,512]{1,0:T(8,128)(2,1)S(1)} %shard_map.37.both_ref), channel_id=1, source_target_pairs={{0,2},{1,7},{2,4},{3,1},{4,6},{5,3},{6,0},{7,5},{8,10},{9,15},{10,... | collective-permute-start | bytes 393224 | tf_op jit(solution)/shard_map/ppermute | solution.py:265
  19.6 6.0 %collective-permute-start.1 = (bf16[128,512]{1,0:T(8,128)(2,1)S(1)}, bf16[128,512]{1,0:T(8,128)(2,1)S(1)}, u32[]{:S(2)}, u32[]{:S(2)}) collective-permute-start(bf16[128,512]{1,0:T(8,128)(2,1)S(1)} %shard_map.37.both_ref), channel_id=1, source_target_pairs={{0,1},{1,0},{2,3},{3,2},{4,5},{5,4},{6,7},{7,6},{8,9},{9,8},{10,11... | collective-permute-start | bytes 393224 | tf_op jit(solution)/shard_map/ppermute | solution.py:303
  21.5 11.3 %collective-permute-start.4 = (bf16[128,512]{1,0:T(8,128)(2,1)S(1)}, bf16[128,512]{1,0:T(8,128)(2,1)S(1)}, u32[]{:S(2)}, u32[]{:S(2)}) collective-permute-start(bf16[128,512]{1,0:T(8,128)(2,1)S(1)} %collective-permute-done.2.refs_0_), channel_id=1, source_target_pairs={{0,2},{1,7},{2,4},{3,1},{4,6},{5,3},{6,0},{7,5},{8,10},{9,15},{10,... | collective-permute-start | bytes 393224 | tf_op jit(solution)/shard_map/ppermute | solution.py:265
  25.6 7.2 %collective-permute-start.3 = (bf16[128,512]{1,0:T(8,128)(2,1)S(1)}, bf16[128,512]{1,0:T(8,128)(2,1)S(1)}, u32[]{:S(2)}, u32[]{:S(2)}) collective-permute-start(bf16[128,512]{1,0:T(8,128)(2,1)S(1)} %collective-permute-done.1.other_ref), channel_id=1, source_target_pairs={{0,2},{1,7},{2,4},{3,1},{4,6},{5,3},{6,0},{7,5},{8,10},{9,15},{10,... | collective-permute-start | bytes 393224 | tf_op jit(solution)/shard_map/ppermute | solution.py:265
  25.6 15.0 %collective-permute-start.8 = (bf16[384,512]{1,0:T(8,128)(2,1)S(1)}, bf16[384,512]{1,0:T(8,128)(2,1)S(1)}, u32[]{:S(2)}, u32[]{:S(2)}) collective-permute-start(bf16[384,512]{1,0:T(8,128)(2,1)S(1)} %bitcast.8), channel_id=1, source_target_pairs={{0,48},{1,193},{2,50},{3,195},{4,52},{5,197},{6,54},{7,199},{8,56}... | collective-permute-start | bytes 1179656 | tf_op jit(solution)/shard_map/ppermute | solution.py:265
  31.7 8.9 %collective-permute-start.7 = (bf16[384,512]{1,0:T(8,128)(2,1)S(1)}, bf16[384,512]{1,0:T(8,128)(2,1)S(1)}, u32[]{:S(2)}, u32[]{:S(2)}) collective-permute-start(bf16[384,512]{1,0:T(8,128)(2,1)S(1)} %bitcast.9), channel_id=1, source_target_pairs={{0,32},{1,129},{2,34},{3,131},{4,36},{5,133},{6,38},{7,135},{8,40}... | collective-permute-start | bytes 1179656 | tf_op jit(solution)/shard_map/ppermute | solution.py:265
  32.2 12.2 %collective-permute-start.6 = (bf16[384,512]{1,0:T(8,128)(2,1)S(1)}, bf16[384,512]{1,0:T(8,128)(2,1)S(1)}, u32[]{:S(2)}, u32[]{:S(2)}) collective-permute-start(bf16[384,512]{1,0:T(8,128)(2,1)S(1)} %bitcast.10), channel_id=1, source_target_pairs={{0,16},{1,65},{2,18},{3,67},{4,20},{5,69},{6,22},{7,71},{8,24},{9,... | collective-permute-start | bytes 1179656 | tf_op jit(solution)/shard_map/ppermute | solution.py:265
  32.8 21.2 %collective-permute-start.5 = (bf16[384,512]{1,0:T(8,128)(2,1)S(1)}, bf16[384,512]{1,0:T(8,128)(2,1)S(1)}, u32[]{:S(2)}, u32[]{:S(2)}) collective-permute-start(bf16[384,512]{1,0:T(8,128)(2,1)S(1)} %shard_map.38.near_ref), channel_id=1, source_target_pairs={{0,1},{1,0},{2,3},{3,2},{4,5},{5,4},{6,7},{7,6},{8,9},{9,8},{10,11... | collective-permute-start | bytes 1179656 | tf_op jit(solution)/shard_map/ppermute | solution.py:307
  45.0 14.0 %collective-permute-start.10 = (bf16[192,512]{1,0:T(8,128)(2,1)S(1)}, bf16[192,512]{1,0:T(8,128)(2,1)S(1)}, u32[]{:S(2)}, u32[]{:S(2)}) collective-permute-start(bf16[192,512]{1,0:T(8,128)(2,1)S(1)} %get-tuple-element.17), channel_id=1, source_target_pairs={{1,0},{2,1},{3,2},{4,3},{5,4},{6,5},{7,6},{9,8},{10,9},{11,10},{12... | collective-permute-start | bytes 589832 | tf_op jit(solution)/shard_map/ppermute | solution.py:311
  52.0 7.0 %collective-permute-start.9 = (bf16[256,512]{1,0:T(8,128)(2,1)S(1)}, bf16[256,512]{1,0:T(8,128)(2,1)S(1)}, u32[]{:S(2)}, u32[]{:S(2)}) collective-permute-start(bf16[256,512]{1,0:T(8,128)(2,1)S(1)} %get-tuple-element.16), channel_id=1, source_target_pairs={{0,1},{1,2},{2,3},{3,4},{4,5},{5,6},{6,7},{8,9},{9,10},{10,11},{11... | collective-permute-start | bytes 786440 | tf_op jit(solution)/shard_map/ppermute | solution.py:310

commit v3 on v1

--- a/solution.py
+++ b/solution.py
@@ -15,7 +15,7 @@
 SIZES = (4, 4, 2, 4, 2)
 
 
-def arrange(slot_a, slot_b, slot_c, slot_d, place_ref, refs, send_left, send_right):
+def arrange(slot_a, slot_b, slot_c, slot_d, place_ref, refs, send_far, send_near):
     core, second = place_ref[1], place_ref[2]
     inner = jnp.where(core == 0, 384, 96)
     outer = jnp.where(core == 0, 96, 384)
@@ -23,21 +23,24 @@
         at = lax.rem(second - s + 4, 4) * outer
         for i in range(4):
             refs[pl.ds(pl.multiple_of(at + i * inner, 96), 96), :] = ref[i * 96:i * 96 + 96, :]
-    send_left[...] = refs[1280:1536, :]
-    send_right[...] = refs[0:192, :]
+    send_far[...] = refs[pl.ds(pl.multiple_of(core * 1280, 256), 256), :]
+    send_near[...] = refs[pl.ds(pl.multiple_of((1 - core) * 1280, 256), 256), :]
+
+
+def score_class(qs, base, rhs, first, count, c):
+    us = range(c, NB, 4)
+    lhs = jnp.concatenate([qs[u * D:(u + 1) * D, :] for u in us], axis=0)
+    s = lax.dot_general(lhs, rhs(c), (((1,), (1,)), ((), ())), preferred_element_type=jnp.float32)
+    s = jnp.tanh(s * DESC ** -0.5)
+    for h in range(count):
+        for n, u in enumerate(us):
+            for v in range(4):
+                base[first + h, v, u] = s[n * D + v * 8:n * D + v * 8 + 8, h * 128:h * 128 + 128]
 
 
 def score_tiles(qs, base, rhs, first, count):
-    scale = DESC ** -0.5
     for c in range(4):
-        us = range(c, NB, 4)
-        lhs = jnp.concatenate([qs[u * D:(u + 1) * D, :] for u in us], axis=0)
-        s = lax.dot_general(lhs, rhs(c), (((1,), (1,)), ((), ())), preferred_element_type=jnp.float32)
-        s = jnp.tanh(s * scale)
-        for h in range(count):
-            for n, u in enumerate(us):
-                for v in range(4):
-                    base[first + h, v, u] = s[n * D + v * 8:n * D + v * 8 + 8, h * 128:h * 128 + 128]
+        score_class(qs, base, rhs, first, count, c)
 
 
 def make_diagonals(base, res, taps_ref, flag_ref, cmask):
@@ -125,7 +128,7 @@
 
         lax.fori_loop(m0, m1, step, 0)
 
-    return diagonals
+    return diagonals, chain
 
 
 def middle(mine_ref, near_ref, far_ref, refs_ref, taps_ref, flag_ref, place_ref, qs, base, res):
@@ -152,21 +155,30 @@
         score_tiles(qs, base, rows(i * 256, 256), 3 + 2 * i, 2)
         return 0
 
-    lax.fori_loop(0, 5, pair, 0)
-    score_tiles(qs, base, rows(1280, 128), 13, 1)
-    make_diagonals(base, res, taps_ref, flag_ref, None)(2, 6, 8, 23, False)
-
-
-def edges(base_in, res_in, qs, refs_ref, left_ref, right_ref, taps_ref, flag_ref,
+    lax.fori_loop(0, 4, pair, 0)
+    diagonals, chain = make_diagonals(base, res, taps_ref, flag_ref, None)
+    for v in range(4):
+        score_class(qs, base, rows(1024, 384), 11, 3, v)
+        chain(2, v, 8, 23, False)
+    diagonals(3, 6, 8, 23, False)
+    diagonals(1, 2, 12, 23, False)
+    diagonals(6, 7, 8, 19, False)
+
+
+def edges(base_in, res_in, qs, refs_ref, far_ref, near_ref, taps_ref, flag_ref, place_ref,
           base, res, o_ref, lo_rows, hi_rows, cmask, sems):
     lo_rows[0:128, :] = jnp.zeros((128, DESC), lo_rows.dtype)
-    lo_rows[128:384, :] = left_ref[...]
+    low = place_ref[1] == 0
+    lo_rows[128:384, :] = jnp.where(low, far_ref[...], near_ref[...])
     lo_rows[384:512, :] = refs_ref[0:128, :]
     hi_rows[0:128, :] = refs_ref[1408:1536, :]
-    hi_rows[128:320, :] = right_ref[...]
+    hi_rows[128:320, :] = jnp.where(low, near_ref[0:192, :], far_ref[0:192, :])
     hi_rows[320:512, :] = jnp.zeros((192, DESC), hi_rows.dtype)
-    for rows, first in ((lo_rows, 0), (hi_rows, 14)):
-        score_tiles(qs, base, lambda c: rows[c * D:c * D + 384, :], first, 3)
+
+    def rows(ref):
+        return lambda c: ref[c * D:c * D + 384, :]
+
+    score_tiles(qs, base, rows(lo_rows), 0, 3)
     j = lax.broadcasted_iota(jnp.int32, (8, 128), 1) - 128
     for t in range(17):
         for c in range(4):
@@ -180,15 +192,18 @@
     def send(m):
         out_copy(m).start()
 
-    diagonals = make_diagonals(base, res, taps_ref, flag_ref, cmask)
-    diagonals(-4, -3, 20, 23, True)
-    diagonals(-3, -2, 16, 23, True)
-    diagonals(-2, -1, 12, 23, True)
+    diagonals, chain = make_diagonals(base, res, taps_ref, flag_ref, cmask)
+    for v in range(4):
+        score_class(qs, base, rows(hi_rows), 14, 3, v)
+        for m in (-4, -3, -2):
+            chain(m, v, 4 - 4 * m, 23, True)
     diagonals(-1, 0, 8, 23, True)
-    diagonals(0, 2, 8, 23, True, send)
+    diagonals(0, 1, 8, 23, True, send)
+    diagonals(1, 2, 8, 11, True, send)
     for n in range(2, 6):
         send(n)
-    diagonals(6, 9, 8, 23, True, send)
+    diagonals(6, 7, 20, 23, True, send)
+    diagonals(7, 9, 8, 23, True, send)
     diagonals(9, 10, 8, 19, True, send)
     diagonals(10, 11, 8, 15, True, send)
     diagonals(11, 12, 8, 11, True, send)
@@ -244,7 +259,7 @@
 
 def run_arrange(slots, place):
     return pl.pallas_call(
-        arrange, out_shape=[rows_of(1536), rows_of(256), rows_of(192)],
+        arrange, out_shape=[rows_of(1536), rows_of(256), rows_of(256)],
         in_specs=[VMEM] * 4 + [SMEM], out_specs=[VMEM] * 3,
         compiler_params=params(8), cost_estimate=cost(0, 3 << 20))(*slots, place)
 
@@ -256,14 +271,14 @@
         compiler_params=params(20), cost_estimate=cost(1 << 32, 12 << 20))(mine, near, far, refs, taps, flags, place)
 
 
-def run_edges(base, res, qs, refs, left, right, taps, flags):
+def run_edges(base, res, qs, refs, far, near, taps, flags, place):
     return pl.pallas_call(
         edges, out_shape=[f32(*BASE), f32(*RES), f32(512, 1536)],
-        in_specs=[VMEM] * 6 + [SMEM] * 2, out_specs=[VMEM] * 2 + [pl.BlockSpec(memory_space=pl.ANY)],
+        in_specs=[VMEM] * 6 + [SMEM] * 3, out_specs=[VMEM] * 2 + [pl.BlockSpec(memory_space=pl.ANY)],
         scratch_shapes=[pltpu.VMEM((512, DESC), jnp.bfloat16), pltpu.VMEM((512, DESC), jnp.bfloat16),
                         pltpu.VMEM((17, 4, 8, 128), jnp.float32), pltpu.SemaphoreType.DMA((12,))],
         input_output_aliases={0: 0, 1: 1},
-        compiler_params=params(20), cost_estimate=cost(1 << 32, 12 << 20))(base, res, qs, refs, left, right, taps, flags)[2]
+        compiler_params=params(20), cost_estimate=cost(1 << 32, 12 << 20))(base, res, qs, refs, far, near, taps, flags, place)[2]
 
 
 def move_rows(value, move):
@@ -290,6 +305,11 @@
 
 def turn(x, y, zl, zh, c):
     return (x, y, zl, (zh + 1 - 2 * c) % 4, c)
+
+
+def across(x, y, zl, zh, c):
+    z = zh - 1 + 2 * c
+    return None if z < 0 or z > 3 else (x, y, zl, z, 1 - c)
 
 
 def first_groups():
@@ -316,11 +336,11 @@
     near = run_pack(near, far)
     far = lax.ppermute(near, "c", [(0, 1), (1, 0)])
     slots = [block] + [move_rows(block, along_second(d)) for d in (1, 2, 3)]
-    refs, send_left, send_right = run_arrange(slots, place)
-    left = lax.ppermute(send_left, ROW, [(i, i + 1) for i in range(7)])
-    right = lax.ppermute(send_right, ROW, [(i + 1, i) for i in range(7)])
+    refs, send_far, send_near = run_arrange(slots, place)
+    rim_far = move_rows(send_far, across)
+    rim_near = lax.ppermute(send_near, "c", [(0, 1), (1, 0)])
     qs, base, res = run_middle(mine, near, far, refs, taps, flags, place)
-    return run_edges(base, res, qs, refs, left, right, taps, flags)
+    return run_edges(base, res, qs, refs, rim_far, rim_near, taps, flags, place)
 
 
 def solution(mesh):

time: 69.5 us -> 67.2 us (0.967)
  starting transfers between devices: 29.9 us -> 28.1 us
    ppermute x2 -> x1, starting transfers between devices: 7.62 us -> 0.09 us  [local(): rim_near = lax.ppermute(send_near, 'c', [(0, 1), (1, 0)])]
    ppermute x6 -> x7, starting transfers between devices: 14.1 us -> 19.8 us  [move_rows(): return lax.ppermute(value, PB + ROW, pairs)]
    ppermute x6 -> x7, waiting for transfers between devices: 23.6 us -> 23.7 us  [move_rows(): return lax.ppermute(value, PB + ROW, pairs)]
  transfers between devices with their start and end apart: 11 -> 11, of which waited for: 5 -> 5; matrix products, arithmetic and copies ran while one was open for 0% -> 0% of each run, Pallas kernels for 8% -> 9%
where the time goes in v3:
time: 67.2 us; the launch traced here: 66.9 us
  starting transfers between devices  28.1 us (42%)
  waiting for transfers between devices  24.6 us (37%)
  Pallas kernels  11.4 us (17%)
  local copies, waits for them, and re-layouts  2.43 us (4%)
    ppermute x7, waiting for transfers between devices, move_rows(): return lax.ppermute(value, PB + ROW, pairs)  23.7 us
    ppermute x7, starting transfers between devices, move_rows(): return lax.ppermute(value, PB + ROW, pairs)  19.8 us
    all_to_all x1, starting transfers between devices, local(): lax.all_to_all(jnp.broadcast_to(r[None], (8, 48, DESC)), PB + ('c',), 0,...  6.36 us
    pallas_call x1, Pallas kernels, run_edges(): pl.pallas_call(edges, out_shape=[f32(*BASE), f32(*RES), f32(512, 1536)],...  5.5 us
    pallas_call x1, Pallas kernels, run_middle(): pl.pallas_call(middle, out_shape=[rows_of(1024), f32(*BASE), f32(*RES)],...  5.17 us
    ppermute x1, starting transfers between devices, local(): mine = run_pack(both, lax.ppermute(both, 'c', [(0, 1), (1, 0)]))  1.73 us
    broadcast_in_dim x1, local copies, waits for them, and re-layouts, local(): jnp.broadcast_to(r[None], (8, 48, DESC))  1.59 us
  transfers between devices with their start and end apart: 11, of which 5 were waited for; matrix products, arithmetic and copies ran while one was open for 0% of the time, Pallas kernels for 9%

profile of v3, /device:TPU:1, one launch (start us, length us, event | category | flops | bytes accessed | tf_op | source)
XLA Modules:
  0.0 66.9 jit_solution(11410081374790216571)
XLA Ops:
  0.0 0.0 copy-start.1
  0.0 1.6 %broadcast_in_dim.2 = bf16[8,48,512]{2,1,0:T(8,128)(2,1)} broadcast(bf16[48,512]{1,0:T(8,128)(2,1)} %param.4), dimensions={1,2} | broadcast | bytes 442368 | tf_op jit(solution)/shard_map/broadcast_in_dim | solution.py:328
  1.6 6.4 %all-to-all-start = ((bf16[8,48,512]{2,1,0:T(8,128)(2,1)}), bf16[8,48,512]{2,1,0:T(8,128)(2,1)S(1)}, u32[]{:S(2)}, u32[]{:S(2)}) async-start(bf16[8,48,512]{2,1,0:T(8,128)(2,1)} %broadcast_in_dim.2), calls=%async_computation | async-start | bytes 786432 | tf_op jit(solution)/shard_map/all_to_all | solution.py:328
  8.0 1.3 %collective-permute-start = (bf16[64,512]{1,0:T(8,128)(2,1)}, bf16[64,512]{1,0:T(8,128)(2,1)S(1)}, u32[]{:S(2)}, u32[]{:S(2)}) collective-permute-start(bf16[64,512]{1,0:T(8,128)(2,1)} %refs_0_.1), channel_id=1, source_target_pairs={{4,12},{5,13},{6,14},{7,15},{8,0},{9,1},{10,2},{11,3},{12,20},{13,... | collective-permute-start | bytes 196616 | tf_op jit(solution)/shard_map/ppermute | solution.py:290
  9.2 6.0 %collective-permute-done.refs_1_ = bf16[64,512]{1,0:T(8,128)(2,1)S(1)} collective-permute-done((bf16[64,512]{1,0:T(8,128)(2,1)}, bf16[64,512]{1,0:T(8,128)(2,1)S(1)}, u32[]{:S(2)}, u32[]{:S(2)}) %collective-permute-start) | collective-permute-done | bytes 65568 | tf_op jit(solution)/shard_map/ppermute | solution.py:290
  15.2 0.0 copy-start
  15.2 0.8 %copy-done = bf16[64,512]{1,0:T(8,128)(2,1)S(1)} copy-done((bf16[64,512]{1,0:T(8,128)(2,1)S(1)}, bf16[64,512]{1,0:T(8,128)(2,1)}, u32[]{:S(2)}) %copy-start) | copy-done | bytes 65560
  16.1 1.7 %collective-permute-start.1 = (bf16[128,512]{1,0:T(8,128)(2,1)S(1)}, bf16[128,512]{1,0:T(8,128)(2,1)S(1)}, u32[]{:S(2)}, u32[]{:S(2)}) collective-permute-start(bf16[128,512]{1,0:T(8,128)(2,1)S(1)} %shard_map.37.refs_0_), channel_id=1, source_target_pairs={{0,1},{1,0},{2,3},{3,2},{4,5},{5,4},{6,7},{7,6},{8,9},{9,8},{10,11... | collective-permute-start | bytes 393224 | tf_op jit(solution)/shard_map/ppermute | solution.py:332
  17.8 1.0 %collective-permute-done.1.refs_1_ = bf16[128,512]{1,0:T(8,128)(2,1)S(1)} collective-permute-done((bf16[128,512]{1,0:T(8,128)(2,1)S(1)}, bf16[128,512]{1,0:T(8,128)(2,1)S(1)}, u32[]{:S(2)}, u32[]{:S(2)}) %collective-permute-start.1) | collective-permute-done | bytes 131104 | tf_op jit(solution)/shard_map/ppermute | solution.py:332
  18.8 3.2 %collective-permute-start.2 = (bf16[256,512]{1,0:T(8,128)(2,1)S(1)}, bf16[256,512]{1,0:T(8,128)(2,1)S(1)}, u32[]{:S(2)}, u32[]{:S(2)}) collective-permute-start(bf16[256,512]{1,0:T(8,128)(2,1)S(1)} %shard_map.38.mine_ref), channel_id=1, source_target_pairs={{0,2},{1,7},{2,4},{3,1},{4,6},{5,3},{6,0},{7,5},{8,10},{9,15},{10,... | collective-permute-start | bytes 786440 | tf_op jit(solution)/shard_map/ppermute | solution.py:290
  22.0 6.5 %collective-permute-done.2.ref.refs_0_ = bf16[256,512]{1,0:T(8,128)(2,1)S(1)} collective-permute-done((bf16[256,512]{1,0:T(8,128)(2,1)S(1)}, bf16[256,512]{1,0:T(8,128)(2,1)S(1)}, u32[]{:S(2)}, u32[]{:S(2)}) %collective-permute-start.2) | collective-permute-done | bytes 262176 | tf_op jit(solution)/shard_map/ppermute | solution.py:290
  28.5 2.4 %collective-permute-start.3 = (bf16[128,512]{1,0:T(8,128)(2,1)S(1)}, bf16[128,512]{1,0:T(8,128)(2,1)S(1)}, u32[]{:S(2)}, u32[]{:S(2)}) collective-permute-start(bf16[128,512]{1,0:T(8,128)(2,1)S(1)} %shard_map.39), channel_id=1, source_target_pairs={{0,2},{1,7},{2,4},{3,1},{4,6},{5,3},{6,0},{7,5},{8,10},{9,15},{10,... | collective-permute-start | bytes 393224 | tf_op jit(solution)/shard_map/ppermute | solution.py:290
  30.9 0.0 all-to-all-done
  30.9 6.4 %collective-permute-start.7 = (bf16[384,512]{1,0:T(8,128)(2,1)S(1)}, bf16[384,512]{1,0:T(8,128)(2,1)S(1)}, u32[]{:S(2)}, u32[]{:S(2)}) collective-permute-start(bf16[384,512]{1,0:T(8,128)(2,1)S(1)} %bitcast.8), channel_id=1, source_target_pairs={{0,48},{1,193},{2,50},{3,195},{4,52},{5,197},{6,54},{7,199},{8,56}... | collective-permute-start | bytes 1179656 | tf_op jit(solution)/shard_map/ppermute | solution.py:290
  37.3 0.3 collective-permute-start.6
  37.6 0.6 collective-permute-start.5
  38.2 0.0 collective-permute-done.3.refs_1_
  38.2 0.1 collective-permute-start.4
  38.3 0.1 pad_add_fusion.place_ref
  38.4 0.1 add_convert_fusion.flag_ref
  38.5 7.8 %collective-permute-done.7.slot_d = bf16[384,512]{1,0:T(8,128)(2,1)S(1)} collective-permute-done((bf16[384,512]{1,0:T(8,128)(2,1)S(1)}, bf16[384,512]{1,0:T(8,128)(2,1)S(1)}, u32[]{:S(2)}, u32[]{:S(2)}) %collective-permute-start.7) | collective-permute-done | bytes 393248 | tf_op jit(solution)/shard_map/ppermute | solution.py:290
  46.3 0.0 collective-permute-done.6.slot_c
  46.3 3.4 %collective-permute-done.5.slot_b = bf16[384,512]{1,0:T(8,128)(2,1)S(1)} collective-permute-done((bf16[384,512]{1,0:T(8,128)(2,1)S(1)}, bf16[384,512]{1,0:T(8,128)(2,1)S(1)}, u32[]{:S(2)}, u32[]{:S(2)}) %collective-permute-start.5) | collective-permute-done | bytes 393248 | tf_op jit(solution)/shard_map/ppermute | solution.py:290
  49.7 0.7 %shard_map.41 = (bf16[1536,512]{1,0:T(8,128)(2,1)S(1)}, bf16[256,512]{1,0:T(8,128)(2,1)S(1)}, bf16[256,512]{1,0:T(8,128)(2,1)S(1)}) custom-call(bf16[384,512]{1,0:T(8,128)(2,1)S(1)} %bitcast.11, bf16[384,512]{1,0:T(8,128)(2,1)S(1)} %collective-permute-done.5.slot_b, bf16[384,512]{1,0:T(8,128)(2,1)S(1)} %collective-permute-done.6.slot_c, ...), custom_call_target="tpu_custom_call" | custom-call | bytes 3145728 | tf_op jit(solution)/shard_map/pallas_call | solution.py:261
  50.3 5.7 %collective-permute-start.8 = (bf16[256,512]{1,0:T(8,128)(2,1)S(1)}, bf16[256,512]{1,0:T(8,128)(2,1)S(1)}, u32[]{:S(2)}, u32[]{:S(2)}) collective-permute-start(bf16[256,512]{1,0:T(8,128)(2,1)S(1)} %get-tuple-element.16), channel_id=1, source_target_pairs={{1,2},{2,1},{3,4},{4,3},{5,6},{6,5},{9,10},{10,9},{11,12},{12,11},... | collective-permute-start | bytes 786440 | tf_op jit(solution)/shard_map/ppermute | solution.py:290
  56.1 0.1 collective-permute-start.9
  56.2 0.0 collective-permute-done.4.far_ref
  56.2 0.0 copy-done.1
  56.2 5.2 %shard_map.42 = (bf16[1024,512]{1,0:T(8,128)(2,1)S(1)}, f32[17,4,30,8,128]{4,3,2,1,0:T(8,128)S(1)}, f32[14,512,128]{2,1,0:T(8,128)S(1)}) custom-call(bf16[256,512]{1,0:T(8,128)(2,1)S(1)} %shard_map.38.mine_ref, bf16[384,512]{1,0:T(8,128)(2,1)S(1)} %shard_map.40.near_ref, bf16[384,512]{1,0:T(8,128)(2,1)S(1)} %collective-permute-done.4.far_ref, ...), custom_call_target="tpu_custom_call" | custom-call | flops 4294967296 | bytes 12582912 | tf_op jit(solution)/shard_map/pallas_call | solution.py:268
  61.3 0.0 collective-permute-done.8.far_ref
  61.4 0.0 collective-permute-done.9.near_ref
  61.4 5.5 %shard_map.43 = (f32[17,4,30,8,128]{4,3,2,1,0:T(8,128)S(1)}, f32[14,512,128]{2,1,0:T(8,128)S(1)}, f32[512,1536]{1,0:T(8,128)}) custom-call(f32[17,4,30,8,128]{4,3,2,1,0:T(8,128)S(1)} %get-tuple-element.13.base_in, f32[14,512,128]{2,1,0:T(8,128)S(1)} %get-tuple-element.14.res_in, ...), custom_call_target="tpu_custom_call", output_to_operand_aliasing={{0}: (0, {}), {1}: (1, {})} | custom-call | flops 4294967296 | bytes 12582912 | tf_op jit(solution)/shard_map/pallas_call | solution.py:275
  (4 shorter events, 0.1 us)
Async XLA Ops:
  0.0 56.2 %copy-start.1 = (f32[2,8]{1,0:T(2,128)S(1)}, f32[2,8]{1,0:T(2,128)}, u32[]{:S(2)}) copy-start(f32[2,8]{1,0:T(2,128)} %taps_ref.3) | copy-start | bytes 196
  1.6 29.3 %all-to-all-start = ((bf16[8,48,512]{2,1,0:T(8,128)(2,1)}), bf16[8,48,512]{2,1,0:T(8,128)(2,1)S(1)}, u32[]{:S(2)}, u32[]{:S(2)}) async-start(bf16[8,48,512]{2,1,0:T(8,128)(2,1)} %broadcast_in_dim.2), calls=%async_computation | async-start | bytes 786432 | tf_op jit(solution)/shard_map/all_to_all | solution.py:328
  8.0 7.3 %collective-permute-start = (bf16[64,512]{1,0:T(8,128)(2,1)}, bf16[64,512]{1,0:T(8,128)(2,1)S(1)}, u32[]{:S(2)}, u32[]{:S(2)}) collective-permute-start(bf16[64,512]{1,0:T(8,128)(2,1)} %refs_0_.1), channel_id=1, source_target_pairs={{4,12},{5,13},{6,14},{7,15},{8,0},{9,1},{10,2},{11,3},{12,20},{13,... | collective-permute-start | bytes 196616 | tf_op jit(solution)/shard_map/ppermute | solution.py:290
  15.2 0.8 %copy-start = (bf16[64,512]{1,0:T(8,128)(2,1)S(1)}, bf16[64,512]{1,0:T(8,128)(2,1)}, u32[]{:S(2)}) copy-start(bf16[64,512]{1,0:T(8,128)(2,1)} %refs_0_.1) | copy-start | bytes 196612
  16.1 2.7 %collective-permute-start.1 = (bf16[128,512]{1,0:T(8,128)(2,1)S(1)}, bf16[128,512]{1,0:T(8,128)(2,1)S(1)}, u32[]{:S(2)}, u32[]{:S(2)}) collective-permute-start(bf16[128,512]{1,0:T(8,128)(2,1)S(1)} %shard_map.37.refs_0_), channel_id=1, source_target_pairs={{0,1},{1,0},{2,3},{3,2},{4,5},{5,4},{6,7},{7,6},{8,9},{9,8},{10,11... | collective-permute-start | bytes 393224 | tf_op jit(solution)/shard_map/ppermute | solution.py:332
  18.8 9.7 %collective-permute-start.2 = (bf16[256,512]{1,0:T(8,128)(2,1)S(1)}, bf16[256,512]{1,0:T(8,128)(2,1)S(1)}, u32[]{:S(2)}, u32[]{:S(2)}) collective-permute-start(bf16[256,512]{1,0:T(8,128)(2,1)S(1)} %shard_map.38.mine_ref), channel_id=1, source_target_pairs={{0,2},{1,7},{2,4},{3,1},{4,6},{5,3},{6,0},{7,5},{8,10},{9,15},{10,... | collective-permute-start | bytes 786440 | tf_op jit(solution)/shard_map/ppermute | solution.py:290
  28.5 9.7 %collective-permute-start.3 = (bf16[128,512]{1,0:T(8,128)(2,1)S(1)}, bf16[128,512]{1,0:T(8,128)(2,1)S(1)}, u32[]{:S(2)}, u32[]{:S(2)}) collective-permute-start(bf16[128,512]{1,0:T(8,128)(2,1)S(1)} %shard_map.39), channel_id=1, source_target_pairs={{0,2},{1,7},{2,4},{3,1},{4,6},{5,3},{6,0},{7,5},{8,10},{9,15},{10,... | collective-permute-start | bytes 393224 | tf_op jit(solution)/shard_map/ppermute | solution.py:290
  30.9 15.4 %collective-permute-start.7 = (bf16[384,512]{1,0:T(8,128)(2,1)S(1)}, bf16[384,512]{1,0:T(8,128)(2,1)S(1)}, u32[]{:S(2)}, u32[]{:S(2)}) collective-permute-start(bf16[384,512]{1,0:T(8,128)(2,1)S(1)} %bitcast.8), channel_id=1, source_target_pairs={{0,48},{1,193},{2,50},{3,195},{4,52},{5,197},{6,54},{7,199},{8,56}... | collective-permute-start | bytes 1179656 | tf_op jit(solution)/shard_map/ppermute | solution.py:290
  37.3 8.9 %collective-permute-start.6 = (bf16[384,512]{1,0:T(8,128)(2,1)S(1)}, bf16[384,512]{1,0:T(8,128)(2,1)S(1)}, u32[]{:S(2)}, u32[]{:S(2)}) collective-permute-start(bf16[384,512]{1,0:T(8,128)(2,1)S(1)} %bitcast.9), channel_id=1, source_target_pairs={{0,32},{1,129},{2,34},{3,131},{4,36},{5,133},{6,38},{7,135},{8,40}... | collective-permute-start | bytes 1179656 | tf_op jit(solution)/shard_map/ppermute | solution.py:290
  37.6 12.1 %collective-permute-start.5 = (bf16[384,512]{1,0:T(8,128)(2,1)S(1)}, bf16[384,512]{1,0:T(8,128)(2,1)S(1)}, u32[]{:S(2)}, u32[]{:S(2)}) collective-permute-start(bf16[384,512]{1,0:T(8,128)(2,1)S(1)} %bitcast.10), channel_id=1, source_target_pairs={{0,16},{1,65},{2,18},{3,67},{4,20},{5,69},{6,22},{7,71},{8,24},{9,... | collective-permute-start | bytes 1179656 | tf_op jit(solution)/shard_map/ppermute | solution.py:290
  38.2 17.9 %collective-permute-start.4 = (bf16[384,512]{1,0:T(8,128)(2,1)S(1)}, bf16[384,512]{1,0:T(8,128)(2,1)S(1)}, u32[]{:S(2)}, u32[]{:S(2)}) collective-permute-start(bf16[384,512]{1,0:T(8,128)(2,1)S(1)} %shard_map.40.near_ref), channel_id=1, source_target_pairs={{0,1},{1,0},{2,3},{3,2},{4,5},{5,4},{6,7},{7,6},{8,9},{9,8},{10,11... | collective-permute-start | bytes 1179656 | tf_op jit(solution)/shard_map/ppermute | solution.py:337
  50.3 11.0 %collective-permute-start.8 = (bf16[256,512]{1,0:T(8,128)(2,1)S(1)}, bf16[256,512]{1,0:T(8,128)(2,1)S(1)}, u32[]{:S(2)}, u32[]{:S(2)}) collective-permute-start(bf16[256,512]{1,0:T(8,128)(2,1)S(1)} %get-tuple-element.16), channel_id=1, source_target_pairs={{1,2},{2,1},{3,4},{4,3},{5,6},{6,5},{9,10},{10,9},{11,12},{12,11},... | collective-permute-start | bytes 786440 | tf_op jit(solution)/shard_map/ppermute | solution.py:290
  56.1 5.3 %collective-permute-start.9 = (bf16[256,512]{1,0:T(8,128)(2,1)S(1)}, bf16[256,512]{1,0:T(8,128)(2,1)S(1)}, u32[]{:S(2)}, u32[]{:S(2)}) collective-permute-start(bf16[256,512]{1,0:T(8,128)(2,1)S(1)} %get-tuple-element.17), channel_id=1, source_target_pairs={{0,1},{1,0},{2,3},{3,2},{4,5},{5,4},{6,7},{7,6},{8,9},{9,8},{10,11... | collective-permute-start | bytes 786440 | tf_op jit(solution)/shard_map/ppermute | solution.py:341
